TPU v7x, 128 devices: a whole 4x4x4 slice. The times are simulated.
128 devices in a mesh: lab: 4 (over y_hi, core), qry: 32 (over z, y_lo, x).
Axes of the slice: x: 4, y: 4 (y_hi: 2, y_lo: 2; y = y_hi * 2 + y_lo), z: 4, core: 2. Of those that a mesh axis runs over, the one named last changes fastest.
Arguments:
- query_hidden: bfloat16 [1024, 3584], P('qry'), may hold values from -6 to 6
- query_proj: bfloat16 [3584, 3584], P('qry', 'lab'), may hold values from -0.09375 to 0.09375
- label_hidden: bfloat16 [32768, 1536], P('qry'), may hold values from -6 to 6
- label_proj: bfloat16 [1536, 3584], P('qry', 'lab'), may hold values from -0.15625 to 0.15625
- pos_ids: int32 [1024, 8], P('qry'), may hold values from 0 to 32767
- pos_count: int32 [1024], P('qry'), may hold values from 1 to 8
Outputs:
- grad_query_proj: float32 [3584, 3584], P('qry', 'lab')
- grad_label_proj: float32 [1536, 3584], P('qry', 'lab')
- label_loss: float32 [32768], P('qry')
- grad_query_embed: float32 [1024, 3584], P('qry', 'lab')
Inputs may be any that keep to these rules, and one draw needn't show every extreme that they name: `pos_ids`: label numbers of the block; only the first pos_count entries of a row are positives, the rest is padding.
All inputs are finite; a program needn't handle non-finite values.
Results may differ from a plain program's by a relative error of at most 0.004.
Values may be sent and summed in bfloat16 or wider, within the bound.
A program may use at most 128 MiB of HBM per device.

v0:
```python
import jax
import jax.numpy as jnp
from jax import lax
from jax.sharding import PartitionSpec as P


def focal_parts(logits, target, counts, temper):
    weight = (1.0 - 0.99) / (1.0 - jnp.power(jnp.float32(0.99), counts + 1.0))
    chance = jax.nn.sigmoid(logits)
    log_pos = -jax.nn.softplus(-logits)
    log_neg = -jax.nn.softplus(logits)
    rest = 1.0 - chance
    loss_terms = -(target * rest * rest * log_pos + (1.0 - target) * chance * chance * log_neg)
    slope = target * (2.0 * chance * rest * rest * log_pos - rest * rest * rest) + (
        1.0 - target
    ) * (chance * chance * chance - 2.0 * chance * chance * rest * log_neg)
    return (weight * loss_terms, (weight * slope * temper).astype(jnp.bfloat16))


def shards(query_hidden, query_proj, label_hidden, label_proj, pos_ids, pos_count):
    width = query_hidden.shape[1]
    temper = width ** (-0.5)
    full_qproj, full_lproj = (
        lax.all_gather(query_proj, "qry", axis=0, tiled=True),
        lax.all_gather(label_proj, "qry", axis=0, tiled=True),
    )
    own_embed = jnp.dot(query_hidden, full_qproj, preferred_element_type=jnp.float32).astype(
        jnp.bfloat16
    )
    all_embed, all_ids, all_count = (
        lax.all_gather(own_embed, "qry", axis=0, tiled=True),
        lax.all_gather(pos_ids, "qry", axis=0, tiled=True),
        lax.all_gather(pos_count, "qry", axis=0, tiled=True),
    )
    label_embed = jnp.dot(label_hidden, full_lproj, preferred_element_type=jnp.float32).astype(
        jnp.bfloat16
    )
    partial_value = lax.dot_general(
        all_embed, label_embed, (((1,), (1,)), ((), ())), preferred_element_type=jnp.float32
    )
    logits = lax.psum(partial_value, "lab") * temper
    n_query = all_embed.shape[0]
    n_label = label_hidden.shape[0]
    offset = lax.axis_index("qry") * n_label
    slot_ids = jnp.arange(pos_ids.shape[1], dtype=jnp.int32)
    in_use = slot_ids[None, :] < all_count[:, None]
    local_ids = all_ids - offset
    columns = jnp.arange(n_label, dtype=jnp.int32)
    matches = (local_ids[:, :, None] == columns[None, None, :]) & in_use[:, :, None]
    counts = jnp.sum(matches.astype(jnp.float32), axis=(0, 1))
    target = jnp.any(matches, axis=1).astype(jnp.float32)
    loss_terms, grad_logits = focal_parts(logits, target, counts[None, :], temper)
    label_loss = jnp.sum(loss_terms, axis=0) / n_query
    grad_label_embed = lax.dot_general(
        grad_logits, all_embed, (((0,), (0,)), ((), ())), preferred_element_type=jnp.float32
    ).astype(jnp.bfloat16)
    embed_total = lax.psum_scatter(
        jnp.dot(grad_logits, label_embed, preferred_element_type=jnp.float32),
        "qry",
        scatter_dimension=0,
        tiled=True,
    )
    grad_query_embed = embed_total.astype(jnp.bfloat16)
    label_part = lax.dot_general(
        label_hidden, grad_label_embed, (((0,), (0,)), ((), ())), preferred_element_type=jnp.float32
    )
    query_part = lax.dot_general(
        query_hidden, grad_query_embed, (((0,), (0,)), ((), ())), preferred_element_type=jnp.float32
    )
    query_total, label_total = (
        lax.psum_scatter(query_part, "qry", scatter_dimension=0, tiled=True),
        lax.psum_scatter(label_part, "qry", scatter_dimension=0, tiled=True),
    )
    return (query_total, label_total, label_loss, embed_total)


def solution(mesh):
    in_specs = (
        P("qry", None),
        P("qry", "lab"),
        P("qry", None),
        P("qry", "lab"),
        P("qry", None),
        P("qry"),
    )
    out_specs = (P("qry", "lab"), P("qry", "lab"), P("qry"), P("qry", "lab"))
    return jax.shard_map(shards, mesh=mesh, in_specs=in_specs, out_specs=out_specs, check_vma=False)
```

profile of v0, /device:TPU:0, one launch (start us, length us, event | category | flops | bytes accessed | tf_op | source)
XLA Modules:
  0.0 1167.7 jit_solution(9398432870501116032)
XLA Ops:
  7.2 0.7 all-gather.5.cloned.1.call-update
  8.0 0.7 all-gather.9.cloned.1.call-update
  8.7 167.0 %all-gather.5.cloned.1.call-done = bf16[3584,896]{1,0:T(8,128)(2,1)} async-done(((bf16[112,896]{1,0:T(8,128)(2,1)}), bf16[3584,896]{1,0:T(8,128)(2,1)}) %all-gather.5.cloned.1.call-update) | async-done | bytes 6422544 | tf_op jit(solution)/shard_map/all_gather | solution.py:24
  175.7 4.7 convolution_convert_fusion.1
  180.5 0.0 all-reduce.3.cloned.1.call-start
  180.5 152.1 %all-gather.9.cloned.1.call-done = bf16[1536,896]{1,0:T(8,128)(2,1)} async-done(((bf16[48,896]{1,0:T(8,128)(2,1)}), bf16[1536,896]{1,0:T(8,128)(2,1)}) %all-gather.9.cloned.1.call-update) | async-done | bytes 2752528 | tf_op jit(solution)/shard_map/all_gather | solution.py:25
  332.6 6.3 convolution_convert_fusion
  338.9 148.4 %all-gather.7.cloned.1.call-done = bf16[1024,896]{1,0:T(8,128)(2,1)} async-done(((bf16[32,896]{1,0:T(8,128)(2,1)}), bf16[1024,896]{1,0:T(8,128)(2,1)}) %all-gather.7.cloned.1.call-update) | async-done | bytes 1835024 | tf_op jit(solution)/shard_map/all_gather | solution.py:31
  487.2 6.4 fusion.25
  493.6 0.0 reduce-scatter.8.cloned.1.call-start
  493.7 0.6 copy-done.3
  494.3 82.5 %all-gather = s32[32,32,8]{1,2,0:T(8,128)S(1)} all-gather(s32[1,32,8]{1,2,0:T(8,128)S(1)} %bitcast.23), channel_id=1, replica_groups=mesh['lab'=4,'qry'=32] {'qry'}, dimensions={0}, use_global_device_ids=true | all-gather | bytes 33792 | tf_op jit(solution)/shard_map/all_gather | solution.py:32
  576.8 1.0 copy.24
  577.9 0.6 dynamic-slice
  579.1 0.2 dynamic-update-slice
  579.4 12.4 %all-reduce = s32[1024]{0:T(1024)S(1)} all-reduce(s32[1024]{0:T(1024)S(1)} %dynamic-update-slice), channel_id=1, replica_groups=mesh['lab'=4,'qry'=32] {'qry'}, use_global_device_ids=true, to_apply=%add | all-reduce | flops 1024 | bytes 8192
  591.8 0.2 iota_compare_fusion.1
  592.0 7.3 convert_reduce_fusion
  599.3 14.2 %fusion.1 = pred[1024,1024]{1,0:T(8,128)(4,1)} fusion(s32[1024,8]{1,0:T(8,128)} %bitcast.22, pred[1024,8]{1,0:T(8,128)(4,1)S(1)} %iota_compare_fusion.1), kind=kLoop, calls=%fused_computation.3 | loop fusion | flops 24117248 | bytes 1089536 | tf_op jit(solution)/shard_map/reduce_or | solution.py:51
  613.5 12.7 %fusion.17 = (f32[1024]{0:T(1024)S(1)}, bf16[1024,1024]{1,0:T(8,128)(2,1)S(1)}) fusion(pred[1024,1024]{1,0:T(8,128)(4,1)} %fusion.1, f32[1024]{0:T(1024)S(1)} %subtract_divide_fusion, f32[1024,1024]{1,0:T(8,128)} %all-reduce.3.cloned.1.call-done), kind=kLoop, calls=%fused_computation.28 | loop fusion | flops 52427776 | bytes 7348224 | tf_op jit(solution)/shard_map/reduce_sum | solution.py:53
  626.2 1.3 copy-done.6
  627.5 4.2 fusion.26
  631.7 0.3 reduce-scatter.12.cloned.1.call-start
  632.0 9.8 convolution_bitcast_fusion.1
  641.8 6.2 copy.27
  648.0 0.0 reduce-scatter.10.cloned.1.call-start
  648.0 152.2 %reduce-scatter.8.cloned.1.call-done = f32[32,896]{1,0:T(8,128)} async-done(((f32[1024,896]{1,0:T(8,128)}), f32[32,896]{1,0:T(8,128)}) %reduce-scatter.8.cloned.1.call-update) | async-done | bytes 114704 | tf_op jit(solution)/shard_map/reduce_scatter | solution.py:57
  800.3 7.4 convolution_bitcast_fusion
  807.6 14.2 %copy.25 = f32[3584,896]{1,0:T(8,128)} copy(f32[3584,896]{0,1:T(8,128)} %convolution_bitcast_fusion) | data formatting | bytes 25690112
  821.9 0.6 broadcast_multiply_fusion
  822.5 149.1 %reduce-scatter.12.cloned.1.call-done = f32[48,896]{1,0:T(8,128)} async-done(((f32[1536,896]{1,0:T(8,128)}), f32[48,896]{1,0:T(8,128)}) %reduce-scatter.12.cloned.1.call-update) | async-done | bytes 172048
  971.5 189.3 %reduce-scatter.10.cloned.1.call-done = f32[112,896]{1,0:T(8,128)} async-done(((f32[3584,896]{1,0:T(8,128)}), f32[112,896]{1,0:T(8,128)}) %reduce-scatter.10.cloned.1.call-update) | async-done | bytes 401424
  (26 shorter events, 0.3 us)
Async XLA Ops:
  7.2 325.4 %copy-start = (bf16[1024,1536]{1,0:T(8,128)(2,1)S(1)}, bf16[1024,1536]{1,0:T(8,128)(2,1)}, u32[]{:S(2)}) copy-start(bf16[1024,1536]{1,0:T(8,128)(2,1)} %param.8) | copy-start | bytes 9437188
  7.2 168.5 %all-gather.5.cloned.1.call-start = ((), (), s32[]{:S(2)}) async-start(), calls=%async_computation.3 | async-start | bytes 6623232 | tf_op jit(solution)/shard_map/all_gather | solution.py:24
  7.9 324.6 %all-gather.9.cloned.1.call-start = ((), (), s32[]{:S(2)}) async-start(), calls=%async_computation.5 | async-start | bytes 2838528 | tf_op jit(solution)/shard_map/all_gather | solution.py:25
  8.7 478.6 %all-gather.7.cloned.1.call-start = ((), (), s32[]{:S(2)}) async-start(), calls=%async_computation.4 | async-start | bytes 1892352 | tf_op jit(solution)/shard_map/all_gather | solution.py:31
  180.5 433.0 %all-reduce.3.cloned.1.call-start = ((), (), s32[]{:S(2)}) async-start(), calls=%async_computation.6 | async-start | bytes 8388608 | tf_op jit(solution)/shard_map/psum | solution.py:41
  493.6 0.7 copy-start.3
  493.6 84.2 %copy-start.5 = (u32[128]{0:T(128)S(1)}, u32[128]{0:T(128)}, u32[]{:S(2)}) copy-start(u32[128]{0:T(128)} %constant.33) | copy-start | bytes 1540
  493.6 85.5 %copy-start.4 = (s32[32]{0:T(128)S(1)}, s32[32]{0:T(128)}, u32[]{:S(2)}) copy-start(s32[32]{0:T(128)} %param.11) | copy-start | bytes 388
  493.6 306.6 %reduce-scatter.8.cloned.1.call-start = ((), (), s32[]{:S(2)}) async-start(), calls=%async_computation.7 | async-start | bytes 3784704 | tf_op jit(solution)/shard_map/reduce_scatter | solution.py:57
  613.5 14.0 %copy-start.7 = (bf16[1024,896]{1,0:T(8,128)(2,1)S(1)}, bf16[1024,896]{1,0:T(8,128)(2,1)}, u32[]{:S(2)}) copy-start(bf16[1024,896]{1,0:T(8,128)(2,1)} %convolution_convert_fusion) | copy-start | bytes 5505028
  626.2 1.3 copy-start.6
  631.7 339.8 %reduce-scatter.12.cloned.1.call-start = ((), (), s32[]{:S(2)}) async-start(), calls=%async_computation.9 | async-start | bytes 5677056
  648.0 152.3 %copy-start.2 = (bf16[32,3584]{1,0:T(8,128)(2,1)S(1)}, bf16[32,3584]{1,0:T(8,128)(2,1)}, u32[]{:S(2)}) copy-start(bf16[32,3584]{1,0:T(8,128)(2,1)} %param.6) | copy-start | bytes 688132
  648.0 512.9 %reduce-scatter.10.cloned.1.call-start = ((), (), s32[]{:S(2)}) async-start(), calls=%async_computation.8 | async-start | bytes 13246464
  821.9 339.0 %copy-start.1 = (bf16[1024,1536]{1,0:T(8,128)(2,1)S(1)}, bf16[1024,1536]{1,0:T(8,128)(2,1)}, u32[]{:S(2)}) copy-start(bf16[1024,1536]{1,0:T(8,128)(2,1)} %param.8) | copy-start | bytes 9437188
Sparse Core Ops, SparseCore 0:
  9.7 165.9 all-gather.4
  177.3 155.1 all-gather.8
  334.8 152.4 all-gather.6
  493.8 93.2 all-reduce.2
  631.8 168.3 reduce-scatter.7
  803.1 168.3 reduce-scatter.11
  974.7 186.1 reduce-scatter.9
where the time goes:
time: 1170 us
  waiting for transfers between devices  959 us (82%)
  blocking collectives  94.9 us (8%)
  matrix products  38.8 us (3%)
  other arithmetic  35 us (3%)
  local copies, waits for them, and re-layouts  24.2 us (2%)
  between operations  14.9 us (1%)
    unnamed x9, waiting for transfers between devices  340 us
    all_gather x1, waiting for transfers between devices, shards(): lax.all_gather(query_proj, 'qry', axis=0, tiled=True)  167 us
    reduce_scatter x1, waiting for transfers between devices, shards(): lax.psum_scatter(jnp.dot(grad_logits, label_embed, preferred_element_type...  152 us
    all_gather x1, waiting for transfers between devices, shards(): lax.all_gather(label_proj, 'qry', axis=0, tiled=True)  152 us
    all_gather x1, waiting for transfers between devices, shards(): lax.all_gather(own_embed, 'qry', axis=0, tiled=True)  148 us
    all_gather x1, blocking collectives, shards(): lax.all_gather(pos_ids, 'qry', axis=0, tiled=True)  82.5 us
  transfers between devices with their start and end apart: 7, of which 6 were waited for; matrix products, arithmetic and copies ran while one was open for 6% of the time, Pallas kernels for 0%

commit v1 on v0

v1 whole, which is shorter than its diff:
```python
import jax
import jax.numpy as jnp
import numpy as np
from jax import lax
from jax.experimental import pallas as pl
from jax.experimental.pallas import tpu as pltpu
from jax.sharding import PartitionSpec as P

NX, NB, NZ, NLAB, NQRY = 4, 8, 4, 4, 32
ROWS = (((0,), (0,)), ((), ()))
COLS = (((1,), (1,)), ((), ()))
MESH = pl.DeviceIdType.MESH
F32, BF16 = jnp.float32, jnp.bfloat16


def push(src, dst, send, recv, **device):
    return pltpu.make_async_remote_copy(
        src_ref=src, dst_ref=dst, send_sem=send, recv_sem=recv, device_id=device, device_id_type=MESH
    )


def dot(left, right, dims=(((1,), (0,)), ((), ()))):
    return lax.dot_general(left, right, dims, preferred_element_type=F32)


def each(count, step):
    def body(d, carry):
        step(d)
        return carry

    lax.fori_loop(1, count, body, 0)


def step_kernel(temper, n_query, qh, qp, lh, lp, ids, gqp_out, glp_out, loss_out, gqe_out, s):
    own = qh.shape[0]
    e_blk, d_blk = qh.shape[1] // NB, lh.shape[1] // NB
    e_row, d_row, width = qp.shape[0], lp.shape[0], qp.shape[1]
    n_label = lh.shape[0]
    quart = NB * own // NLAB
    here = NB * own
    d_pair = 2 * d_blk
    me, j = lax.axis_index("qry"), lax.axis_index("lab")
    x, b, z = lax.rem(me, NX), lax.div(me, NX), lax.div(me, 2 * NX)
    y = lax.rem(b, 2)
    y_peer = (2 * z + 1 - y) * NX + x

    def at_b(d):
        nb = lax.rem(b + d, NB)
        return nb, nb * NX + x

    def at_x(d):
        nx = lax.rem(x + d, NX)
        return nx, b * NX + nx

    def at_plane(d):
        nx, nz = lax.rem(x + lax.rem(d, NX), NX), lax.rem(z + lax.div(d, NX), NZ)
        return nx, nz, (2 * nz + y) * NX + nx

    def at_lab(d):
        return lax.rem(j + d, NLAB)

    def rows(index, size):
        return pl.ds(pl.multiple_of(index * size, size), size)

    fetch = pltpu.make_async_copy(lh, s.lh, s.fetch)
    fetch.start()
    for k in range(NB):
        s.q_send[k] = qh[:, k * e_blk : (k + 1) * e_blk]

    barrier = pltpu.get_barrier_semaphore()
    each(NQRY, lambda d: pl.semaphore_signal(barrier, inc=1, device_id={"qry": lax.rem(me + d, NQRY)}, device_id_type=MESH))
    each(NLAB, lambda d: pl.semaphore_signal(barrier, inc=1, device_id={"lab": at_lab(d)}, device_id_type=MESH))
    pl.semaphore_wait(barrier, NQRY - 1 + NLAB - 1)

    def hidden(d):
        nb, dev = at_b(d)
        return push(s.q_send.at[nb], s.q_blk.at[b], s.ss_a.at[d], s.rs_a.at[d], qry=dev)

    def q_rows(d):
        return push(qp, s.qp.at[rows(x, e_row)], s.ss_w.at[d], s.rs_w.at[d], qry=at_x(d)[1])

    def l_rows(d):
        return push(lp, s.lp.at[rows(x, d_row)], s.ss_d.at[d], s.rs_d.at[d], qry=at_x(d)[1])

    mine = 2 * x + y

    def positives(d):
        return push(ids, s.ids.at[mine], s.ss_i.at[d], s.rs_i.at[mine], qry=lax.rem(me + d, NQRY))

    each(NB, lambda d: hidden(d).start())
    each(NX, lambda d: q_rows(d).start())

    @pl.when(z == j)
    def _():
        each(NQRY, lambda d: positives(d).start())
        s.ids[mine] = ids[...]

    each(NX, lambda d: l_rows(d).start())
    s.q_blk[b] = s.q_send[b]
    s.qp[rows(x, e_row), :] = qp[...]
    s.lp[rows(x, d_row), :] = lp[...]

    each(NB, lambda d: hidden(d).wait_recv())
    each(NX, lambda d: q_rows(d).wait_recv())
    q_blk = s.q_blk[...].reshape(here, e_blk)
    s.q_part[...] = dot(q_blk, s.qp[...]).reshape(NB, own, width)

    def q_sum(d):
        nb, dev = at_b(d)
        return push(s.q_part.at[nb], s.q_recv.at[b], s.ss_b.at[d], s.rs_b.at[d], qry=dev)

    each(NB, lambda d: q_sum(d).start())
    s.q_recv[b] = s.q_part[b]

    def id_wait(k):
        push(ids, s.ids.at[k], s.ss_i.at[0], s.rs_i.at[k], qry=y_peer).wait_recv()

    for k in range(NB):

        @pl.when(jnp.logical_or(z != j, mine != k))
        def _():
            id_wait(k)

    local = s.ids[...].reshape(here, ids.shape[1]) - n_label * me
    wide = 256
    for c in range(n_label // wide):
        column = lax.broadcasted_iota(jnp.int32, (here, wide), 1) + c * wide
        found = jnp.zeros((here, wide), F32)
        for slot in range(ids.shape[1]):
            found += jnp.where(local[:, slot : slot + 1] == column, 1.0, 0.0)
        s.mask[:, c * wide : (c + 1) * wide] = found
        s.c_part[:, c * wide : (c + 1) * wide] = jnp.sum(found.reshape(here // 8, 8, wide), axis=0)

    def count(d):
        return push(s.c_part, s.c_recv.at[j], s.ss_c.at[d], s.rs_c.at[d], lab=at_lab(d))

    each(NLAB, lambda d: count(d).start())
    s.c_recv[j] = s.c_part[...]

    each(NB, lambda d: q_sum(d).wait_recv())
    total = s.q_recv[0]
    for k in range(1, NB):
        total += s.q_recv[k]
    s.qe[b] = total.astype(BF16)

    def q_all(d):
        return push(s.qe.at[b], s.qe.at[b], s.ss_e.at[d], s.rs_e.at[d], qry=at_b(d)[1])

    each(NB, lambda d: q_all(d).start())
    each(NX, lambda d: l_rows(d).wait_recv())
    each(NB, lambda d: q_all(d).wait_recv())

    qe = s.qe[...].reshape(here, width)
    s.t_part[...] = dot(qe, s.lp[...], COLS).reshape(NLAB, quart, d_blk)

    def t_sum(d):
        nj = at_lab(d)
        return push(s.t_part.at[nj], s.t_recv.at[j], s.ss_t.at[d], s.rs_t.at[d], lab=nj)

    each(NLAB, lambda d: t_sum(d).start())
    s.t_recv[j] = s.t_part[j]

    each(NLAB, lambda d: count(d).wait_recv())
    counts = jnp.sum(s.c_recv[0] + s.c_recv[1] + s.c_recv[2] + s.c_recv[3], axis=0, keepdims=True)
    s.weight[...] = (1.0 - 0.99) / (1.0 - jnp.exp((counts + 1.0) * float(np.log(np.float64(np.float32(0.99))))))

    each(NLAB, lambda d: t_sum(d).wait_recv())
    s.t_own[...] = (s.t_recv[0] + s.t_recv[1] + s.t_recv[2] + s.t_recv[3]).astype(BF16)
    t_swap = push(s.t_own, s.t_peer, s.ss_ty, s.rs_ty, qry=y_peer)
    t_swap.start()
    t_swap.wait_recv()

    @pl.when(y == 0)
    def _():
        s.t_pair[:, :d_blk] = s.t_own[...]
        s.t_pair[:, d_blk:] = s.t_peer[...]

    @pl.when(y == 1)
    def _():
        s.t_pair[:, :d_blk] = s.t_peer[...]
        s.t_pair[:, d_blk:] = s.t_own[...]

    def t_all(d):
        return push(
            s.t_pair, s.t.at[rows(x, quart), rows(z, d_pair)], s.ss_p.at[d], s.rs_p.at[d], qry=at_plane(d)[2]
        )

    each(NX * NZ, lambda d: t_all(d).start())
    s.t[rows(x, quart), rows(z, d_pair)] = s.t_pair[...]
    fetch.wait()
    each(NX * NZ, lambda d: t_all(d).wait_recv())

    tall = 32

    def label_block(c, carry):
        cols = rows(c, wide)
        s.logit[...] = dot(s.t[...], s.lh[cols, :], COLS) * temper
        weight = s.weight[:, cols]

        def row_block(r, loss):
            at = rows(r, tall)
            value = s.logit[at, :]
            hit = s.mask[at, cols] > 0.0
            value = jnp.where(hit, -value, value)
            small = jnp.exp(-jnp.abs(value))
            soft = jnp.maximum(value, 0.0) + jnp.log1p(small)
            over = 1.0 / (1.0 + small)
            under = small * over
            high = value >= 0.0
            chance, rest = jnp.where(high, over, under), jnp.where(high, under, over)
            square = chance * chance
            slope = weight * (square * (chance + 2.0 * rest * soft)) * temper
            s.gl[at, cols] = jnp.where(hit, -slope, slope).astype(BF16)
            return loss + jnp.sum((weight * (square * soft)).reshape(tall // 8, 8, wide), axis=0)

        s.l_part[:, cols] = lax.fori_loop(0, here // tall, row_block, jnp.zeros((8, wide), F32))
        return carry

    lax.fori_loop(0, n_label // wide, label_block, 0)

    spot = NX * z + x

    def u_sum(d):
        nx, nz, dev = at_plane(d)
        return push(s.u_part.at[rows(nx, quart), rows(nz, d_pair)], s.u_recv.at[spot], s.ss_u.at[d], s.rs_u.at[d], qry=dev)

    def u_block(k, carry):
        dz = lax.rem(k + 1, NZ)
        cols = rows(lax.rem(z + dz, NZ), d_pair)
        s.u_part[:, cols] = dot(s.gl[...], s.lh[:, cols]).astype(BF16)

        def send(dx, inner):
            @pl.when(dz * NX + dx > 0)
            def _():
                u_sum(dz * NX + dx).start()

            return inner

        lax.fori_loop(0, NX, send, 0)
        return carry

    lax.fori_loop(0, NZ, u_block, 0)

    def loss_sum(d):
        return push(s.l_part, s.l_recv.at[j], s.ss_l.at[d], s.rs_l.at[d], lab=at_lab(d))

    each(NLAB, lambda d: loss_sum(d).start())
    s.l_recv[j] = s.l_part[...]
    s.u_recv[spot] = s.u_part[rows(x, quart), rows(z, d_pair)]
    each(NX * NZ, lambda d: u_sum(d).wait_recv())
    back = s.u_recv[0].astype(F32)
    for k in range(1, NX * NZ):
        back += s.u_recv[k].astype(F32)

    @pl.when(y == 0)
    def _():
        s.u_keep[...] = back[:, :d_blk]
        s.u_give[...] = back[:, d_blk:]

    @pl.when(y == 1)
    def _():
        s.u_keep[...] = back[:, d_blk:]
        s.u_give[...] = back[:, :d_blk]

    u_swap = push(s.u_give, s.u_peer, s.ss_uy, s.rs_uy, qry=y_peer)
    u_swap.start()
    u_swap.wait_recv()
    s.u[j] = (s.u_keep[...] + s.u_peer[...]).astype(BF16)

    def u_all(d):
        return push(s.u.at[j], s.u.at[j], s.ss_v.at[d], s.rs_v.at[d], lab=at_lab(d))

    each(NLAB, lambda d: u_all(d).start())
    each(NLAB, lambda d: u_all(d).wait_recv())
    u = s.u[...].reshape(here, d_blk)

    part = dot(u, s.lp[...]).reshape(NB, own, width)
    s.g_part[...] = part
    s.g_send[...] = part.astype(BF16)

    def g_sum(d):
        nb, dev = at_b(d)
        return push(s.g_send.at[nb], s.g_recv.at[b], s.ss_g.at[d], s.rs_g.at[d], qry=dev)

    each(NB, lambda d: g_sum(d).start())
    part = dot(u, qe, ROWS).reshape(NX, d_row, width)
    s.k_part[...] = part
    s.k_send[...] = part.astype(BF16)

    def k_sum(d):
        nx, dev = at_x(d)
        return push(s.k_send.at[nx], s.k_recv.at[x], s.ss_k.at[d], s.rs_k.at[d], qry=dev)

    each(NX, lambda d: k_sum(d).start())
    each(NB, lambda d: g_sum(d).wait_recv())
    total = s.g_part[b]
    for d in range(1, NB):
        total += s.g_recv[lax.rem(b + d, NB)].astype(F32)
    gqe_out[...] = total
    s.ge[b] = total.astype(BF16)

    def g_all(d):
        return push(s.ge.at[b], s.ge.at[b], s.ss_h.at[d], s.rs_h.at[d], qry=at_b(d)[1])

    each(NB, lambda d: g_all(d).start())
    each(NLAB, lambda d: loss_sum(d).wait_recv())
    losses = jnp.sum(s.l_recv[0] + s.l_recv[1] + s.l_recv[2] + s.l_recv[3], axis=0, keepdims=True)
    loss_out[...] = losses / n_query
    each(NX, lambda d: k_sum(d).wait_recv())
    total = s.k_part[x]
    for d in range(1, NX):
        total += s.k_recv[lax.rem(x + d, NX)].astype(F32)
    glp_out[...] = total

    each(NB, lambda d: g_all(d).wait_recv())
    part = dot(s.q_blk[...].reshape(here, e_blk), s.ge[...].reshape(here, width), ROWS).reshape(NX, e_row, width)
    s.p_part[...] = part
    s.p_send[...] = part.astype(BF16)

    def p_sum(d):
        nx, dev = at_x(d)
        return push(s.p_send.at[nx], s.p_recv.at[x], s.ss_q.at[d], s.rs_q.at[d], qry=dev)

    each(NX, lambda d: p_sum(d).start())
    each(NX, lambda d: p_sum(d).wait_recv())
    total = s.p_part[x]
    for d in range(1, NX):
        total += s.p_recv[lax.rem(x + d, NX)].astype(F32)
    gqp_out[...] = total

    for copies in (hidden, q_sum, q_all, g_sum, g_all):
        each(NB, lambda d: copies(d).wait_send())
    for copies in (q_rows, l_rows, k_sum, p_sum):
        each(NX, lambda d: copies(d).wait_send())
    for copies in (count, t_sum, u_all, loss_sum):
        each(NLAB, lambda d: copies(d).wait_send())
    for copies in (t_all, u_sum):
        each(NX * NZ, lambda d: copies(d).wait_send())
    t_swap.wait_send()
    u_swap.wait_send()

    @pl.when(z == j)
    def _():
        each(NQRY, lambda d: positives(d).wait_send())


class Scratch:
    def __init__(self, names, refs):
        for name, ref in zip(names, refs):
            setattr(self, name, ref)


def shards(query_hidden, query_proj, label_hidden, label_proj, pos_ids, pos_count):
    own, wide_e = query_hidden.shape
    n_label, wide_d = label_hidden.shape
    e_row, width = query_proj.shape
    d_row = label_proj.shape[0]
    slots = pos_ids.shape[1]
    e_blk, d_blk = wide_e // NB, wide_d // NB
    here, quart = NB * own, NB * own // NLAB
    used = jnp.arange(slots, dtype=jnp.int32)[None, :] < pos_count[:, None]
    ids = jnp.where(used, pos_ids, -1)
    vmem, dma = pltpu.VMEM, pltpu.SemaphoreType.DMA
    scratch = {
        "lh": vmem((n_label, wide_d), BF16),
        "q_send": vmem((NB, own, e_blk), BF16),
        "q_blk": vmem((NB, own, e_blk), BF16),
        "qp": vmem((NX * e_row, width), BF16),
        "lp": vmem((NX * d_row, width), BF16),
        "ids": vmem((NB, own, slots), jnp.int32),
        "mask": vmem((here, n_label), F32),
        "c_part": vmem((8, n_label), F32),
        "c_recv": vmem((NLAB, 8, n_label), F32),
        "weight": vmem((1, n_label), F32),
        "q_part": vmem((NB, own, width), F32),
        "q_recv": vmem((NB, own, width), F32),
        "qe": vmem((NB, own, width), BF16),
        "t_part": vmem((NLAB, quart, d_blk), F32),
        "t_recv": vmem((NLAB, quart, d_blk), F32),
        "t_own": vmem((quart, d_blk), BF16),
        "t_peer": vmem((quart, d_blk), BF16),
        "t_pair": vmem((quart, 2 * d_blk), BF16),
        "t": vmem((here, wide_d), BF16),
        "logit": vmem((here, 256), F32),
        "gl": vmem((here, n_label), BF16),
        "l_part": vmem((8, n_label), F32),
        "l_recv": vmem((NLAB, 8, n_label), F32),
        "u_part": vmem((here, wide_d), BF16),
        "u_recv": vmem((NX * NZ, quart, 2 * d_blk), BF16),
        "u_keep": vmem((quart, d_blk), F32),
        "u_give": vmem((quart, d_blk), F32),
        "u_peer": vmem((quart, d_blk), F32),
        "u": vmem((NLAB, quart, d_blk), BF16),
        "g_part": vmem((NB, own, width), F32),
        "g_send": vmem((NB, own, width), BF16),
        "g_recv": vmem((NB, own, width), BF16),
        "ge": vmem((NB, own, width), BF16),
        "k_part": vmem((NX, d_row, width), F32),
        "k_send": vmem((NX, d_row, width), BF16),
        "k_recv": vmem((NX, d_row, width), BF16),
        "p_part": vmem((NX, e_row, width), F32),
        "p_send": vmem((NX, e_row, width), BF16),
        "p_recv": vmem((NX, e_row, width), BF16),
        "fetch": dma(()),
    }
    for name, count in (
        ("a", NB), ("w", NX), ("d", NX), ("b", NB), ("e", NB), ("c", NLAB), ("t", NLAB), ("p", NX * NZ), ("u", NX * NZ),
        ("v", NLAB), ("l", NLAB), ("g", NB), ("h", NB), ("k", NX), ("q", NX),
    ):
        scratch["ss_" + name] = dma((count,))
        scratch["rs_" + name] = dma((count,))
    scratch["ss_i"], scratch["rs_i"] = dma((NQRY,)), dma((NB,))
    for name in ("ss_ty", "rs_ty", "ss_uy", "rs_uy"):
        scratch[name] = dma(())
    names = tuple(scratch)
    in_vmem = pl.BlockSpec(memory_space=pltpu.VMEM)

    def kernel(*refs):
        step_kernel(wide_e ** (-0.5), NQRY * own, *refs[:9], Scratch(names, refs[9:]))

    gqp, glp, loss, gqe = pl.pallas_call(
        kernel,
        out_shape=(
            jax.ShapeDtypeStruct((e_row, width), F32),
            jax.ShapeDtypeStruct((d_row, width), F32),
            jax.ShapeDtypeStruct((1, n_label), F32),
            jax.ShapeDtypeStruct((own, width), F32),
        ),
        in_specs=[in_vmem, in_vmem, pl.BlockSpec(memory_space=pl.ANY), in_vmem, in_vmem],
        out_specs=(in_vmem,) * 4,
        scratch_shapes=list(scratch.values()),
        compiler_params=pltpu.CompilerParams(
            collective_id=0, has_side_effects=True, vmem_limit_bytes=48 << 20
        ),
        name="focal_step",
    )(query_hidden, query_proj, label_hidden, label_proj, ids)
    return gqp, glp, loss.reshape(n_label), gqe


def solution(mesh):
    in_specs = (
        P("qry", None),
        P("qry", "lab"),
        P("qry", None),
        P("qry", "lab"),
        P("qry", None),
        P("qry"),
    )
    out_specs = (P("qry", "lab"), P("qry", "lab"), P("qry"), P("qry", "lab"))
    return jax.shard_map(shards, mesh=mesh, in_specs=in_specs, out_specs=out_specs, check_vma=False)
```

time: 1170 us -> 122 us (0.10)
  waiting for transfers between devices: 959 us -> 0 us
  Pallas kernels: 0 us -> 111 us
  blocking collectives: 94.9 us -> 0 us
  matrix products: 38.8 us -> 0 us
  other arithmetic: 35 us -> 0.73 us
  local copies, waits for them, and re-layouts: 24.2 us -> 8.06 us
  between operations: 14.9 us -> 0.65 us
    all_gather x3 -> x0, waiting for transfers between devices: 467 us -> none  [the longest x1 167 us: shards(): lax.all_gather(query_proj, 'qry', axis=0, tiled=True)]
    unnamed x9 -> x0, waiting for transfers between devices: 340 us -> none
    reduce_scatter x1 -> x0, waiting for transfers between devices: 152 us -> none  [shards(): lax.psum_scatter(jnp.dot(grad_logits, label_embed, preferred_element_type...]
    pallas_call x0 -> x1, Pallas kernels: none -> 111 us  [shards(): pl.pallas_call(kernel, out_shape=(jax.ShapeDtypeStruct((e_row, width), F3...]
    all_gather x1 -> x0, blocking collectives: 82.5 us -> none  [shards(): lax.all_gather(pos_ids, 'qry', axis=0, tiled=True)]
    dot_general x6 -> x0, matrix products: 38.8 us -> none  [the longest x1 9.79 us: shards(): lax.dot_general(label_hidden, grad_label_embed, (((0,), (0,)), ((), ())),...]
    reduce_sum x2 -> x0, other arithmetic: 20 us -> none  [the longest x1 12.7 us: shards(): label_loss = jnp.sum(loss_terms, axis=0) / n_query]
    unnamed x21 -> x13, local copies, waits for them, and re-layouts: 23.2 us -> 8.06 us
  transfers between devices with their start and end apart: 7 -> 0, of which waited for: 6 -> 0; matrix products, arithmetic and copies ran while one was open for 6% -> 0% of each run, Pallas kernels for 0% -> 0%
where the time goes in v1:
time: 122 us; the launch traced here: 121 us
  Pallas kernels  111 us (91%)
  local copies, waits for them, and re-layouts  8.06 us (7%)
    pallas_call x1, Pallas kernels, shards(): pl.pallas_call(kernel, out_shape=(jax.ShapeDtypeStruct((e_row, width), F3...  111 us
    unnamed x13, local copies, waits for them, and re-layouts  8.06 us

profile of v1, /device:TPU:0, one launch (start us, length us, event | category | flops | bytes accessed | tf_op | source)
XLA Modules:
  0.0 120.7 jit_solution(4090332531757244741)
XLA Ops:
  0.6 0.8 copy.10
  1.4 0.7 fusion.refs_4_
  2.1 0.0 copy-start
  2.1 1.9 %copy-done = bf16[1024,1536]{1,0:T(8,128)(2,1)S(1)} copy-done((bf16[1024,1536]{1,0:T(8,128)(2,1)S(1)}, bf16[1024,1536]{1,0:T(8,128)(2,1)}, u32[]{:S(2)}) %copy-start) | copy-done | bytes 3145752
  4.0 0.0 copy-start.1
  4.0 0.9 copy-done.1
  4.9 0.0 copy-start.2
  5.0 0.9 copy-done.2
  5.9 0.0 copy-start.3
  5.9 0.9 copy-done.3
  6.8 111.2 %focal_step.1 = (f32[112,896]{1,0:T(8,128)S(1)}, f32[48,896]{1,0:T(8,128)S(1)}, f32[1,1024]{1,0:T(1,128)S(1)}, f32[32,896]{1,0:T(8,128)S(1)}) custom-call(bf16[32,3584]{1,0:T(8,128)(2,1)S(1)} %copy-done.1, bf16[112,896]{1,0:T(8,128)(2,1)S(1)} %copy-done.2, bf16[1024,1536]{1,0:T(8,128)(2,1)S(1)} %copy-done, bf16[48,896]{1,0:T(8,128)(2,1)S(1)} %copy-done.3, ...), custom_call_target="tpu_custom_call" | custom-call | tf_op jit(solution)/shard_map/focal_step/pallas_call | solution.py:421
  118.0 0.8 copy.15
  118.8 0.7 copy.16
  119.4 0.6 copy.17
  120.0 0.6 copy.18
Async XLA Ops:
  2.1 1.9 %copy-start = (bf16[1024,1536]{1,0:T(8,128)(2,1)S(1)}, bf16[1024,1536]{1,0:T(8,128)(2,1)}, u32[]{:S(2)}) copy-start(bf16[1024,1536]{1,0:T(8,128)(2,1)} %refs_2_.1) | copy-start | bytes 9437188
  4.0 0.9 copy-start.1
  4.9 0.9 copy-start.2
  5.9 0.9 copy-start.3

commit v2 on v1

v2 whole, which is shorter than its diff:
```python
import jax
import jax.numpy as jnp
import numpy as np
from jax import lax
from jax.experimental import pallas as pl
from jax.experimental.pallas import tpu as pltpu
from jax.sharding import PartitionSpec as P

NX, NB, NZ, NLAB, NQRY = 4, 8, 4, 4, 32
ROWS = (((0,), (0,)), ((), ()))
COLS = (((1,), (1,)), ((), ()))
MESH = pl.DeviceIdType.MESH
F32, BF16 = jnp.float32, jnp.bfloat16


def push(src, dst, send, recv, **device):
    return pltpu.make_async_remote_copy(
        src_ref=src, dst_ref=dst, send_sem=send, recv_sem=recv, device_id=device, device_id_type=MESH
    )


def dot(left, right, dims=(((1,), (0,)), ((), ()))):
    return lax.dot_general(left, right, dims, preferred_element_type=F32)


def each(count, step):
    def body(d, carry):
        step(d)
        return carry

    lax.fori_loop(1, count, body, 0)


def step_kernel(temper, n_query, qh, qp, lh, lp, ids, used, gqp_out, glp_out, loss_out, gqe_out, s):
    own = qh.shape[0]
    e_blk, d_blk = qh.shape[1] // NB, lh.shape[1] // NB
    e_row, d_row, width = qp.shape[0], lp.shape[0], qp.shape[1]
    n_label = lh.shape[0]
    quart = NB * own // NLAB
    here = NB * own
    d_pair = 2 * d_blk
    me, j = lax.axis_index("qry"), lax.axis_index("lab")
    x, b, z = lax.rem(me, NX), lax.div(me, NX), lax.div(me, 2 * NX)
    y = lax.rem(b, 2)
    y_peer = (2 * z + 1 - y) * NX + x

    def at_b(d):
        nb = lax.rem(b + d, NB)
        return nb, nb * NX + x

    def at_x(d):
        nx = lax.rem(x + d, NX)
        return nx, b * NX + nx

    def at_z(d):
        nz = lax.rem(z + d, NZ)
        return nz, (2 * nz + y) * NX + x

    def at_plane(d):
        nx, nz = lax.rem(x + lax.rem(d, NX), NX), lax.rem(z + lax.div(d, NX), NZ)
        return nx, nz, (2 * nz + y) * NX + nx

    def at_lab(d):
        return lax.rem(j + d, NLAB)

    def rows(index, size):
        return pl.ds(pl.multiple_of(index * size, size), size)

    sent = []

    def start(count, copies):
        each(count, lambda d: copies(d).start())
        sent.append((count, copies))

    def arrive(count, copies):
        each(count, lambda d: copies(d).wait_recv())

    loads = [
        pltpu.make_async_copy(source, target, s.load.at[k])
        for k, (source, target) in enumerate(
            (
                (qh, s.qh),
                (ids, s.ids_raw),
                (used, s.used),
                (qp, s.qp.at[rows(x, e_row)]),
                (lp, s.lp.at[rows(x, d_row)]),
                (lh, s.lh),
            )
        )
    ]
    for load in loads:
        load.start()

    barrier = pltpu.get_barrier_semaphore()
    each(NX * NZ, lambda d: pl.semaphore_signal(barrier, inc=1, device_id={"qry": at_plane(d)[2]}, device_id_type=MESH))
    for d in range(1, NB, 2):
        pl.semaphore_signal(barrier, inc=1, device_id={"qry": at_b(d)[1]}, device_id_type=MESH)
    each(NLAB, lambda d: pl.semaphore_signal(barrier, inc=1, device_id={"lab": at_lab(d)}, device_id_type=MESH))
    loads[0].wait()
    for k in range(NB):
        s.q_send[k] = s.qh[:, k * e_blk : (k + 1) * e_blk]
    loads[1].wait()
    loads[2].wait()
    slots = ids.shape[0]
    s.ids_send[...] = jnp.full(s.ids_send.shape, -1, jnp.int32)
    slot_at = lax.broadcasted_iota(jnp.int32, ids.shape, 0)
    s.ids_send[:, :own] = jnp.where(slot_at < s.used[...], s.ids_raw[...], -1)
    pl.semaphore_wait(barrier, NX * NZ - 1 + NB // 2 + NLAB - 1)

    def hidden(d):
        nb, dev = at_b(d)
        return push(s.q_send.at[nb], s.q_blk.at[b], s.ss_a.at[d], s.rs_a.at[d], qry=dev)

    def q_rows(d):
        return push(qp, s.qp.at[rows(x, e_row)], s.ss_w.at[d], s.rs_w.at[d], qry=at_x(d)[1])

    def l_rows(d):
        return push(lp, s.lp.at[rows(x, d_row)], s.ss_d.at[d], s.rs_d.at[d], qry=at_x(d)[1])

    mine = 2 * x + y
    ids_swap = push(s.ids_send, s.ids.at[mine], s.ss_iy, s.rs_iy, qry=y_peer)

    def positives(d):
        return push(
            s.ids.at[pl.ds(2 * x, 2)], s.ids.at[pl.ds(2 * x, 2)], s.ss_i.at[d], s.rs_i.at[x], qry=at_plane(d)[2]
        )

    start(NB, hidden)
    start(NX, q_rows)

    @pl.when(z == j)
    def _():
        ids_swap.start()
        s.ids[mine] = s.ids_send[...]
        ids_swap.wait_recv()
        each(NX * NZ, lambda d: positives(d).start())

    def ids_arrive():
        for k in range(NX):

            @pl.when(jnp.logical_or(z != j, x != k))
            def _():
                pair = s.ids.at[pl.ds(2 * k, 2)]
                push(pair, pair, s.ss_i.at[0], s.rs_i.at[k], qry=y_peer).wait_recv()

    def ids_sent():
        @pl.when(z == j)
        def _():
            ids_swap.wait_send()
            each(NX * NZ, lambda d: positives(d).wait_send())

    s.q_blk[b] = s.q_send[b]
    loads[3].wait()

    arrive(NB, hidden)
    arrive(NX, q_rows)
    start(NX, l_rows)
    q_blk = s.q_blk[...].reshape(here, e_blk)
    s.q_part[...] = dot(q_blk, s.qp[...]).reshape(NB, own, width)

    def q_sum(d):
        nb, dev = at_b(d)
        return push(s.q_part.at[nb], s.q_recv.at[b], s.ss_b.at[d], s.rs_b.at[d], qry=dev)

    start(NB, q_sum)
    s.q_recv[b] = s.q_part[b]

    ids_arrive()
    local = s.ids[...].reshape(NB * slots, s.ids.shape[2]).T - n_label * me
    wide = 256
    for c in range(n_label // wide):
        column = lax.broadcasted_iota(jnp.int32, (own, wide), 1) + c * wide
        tally = jnp.zeros((8, wide), F32)
        for k in range(NB):
            found = jnp.zeros((own, wide), F32)
            for slot in range(k * slots, (k + 1) * slots):
                found += jnp.where(local[:own, slot : slot + 1] == column, 1.0, 0.0)
            s.mask[k * own : (k + 1) * own, c * wide : (c + 1) * wide] = found
            tally += jnp.sum(found.reshape(own // 8, 8, wide), axis=0)
        s.c_part[:, c * wide : (c + 1) * wide] = tally

    def count(d):
        return push(s.c_part, s.c_recv.at[j], s.ss_c.at[d], s.rs_c.at[d], lab=at_lab(d))

    start(NLAB, count)
    s.c_recv[j] = s.c_part[...]

    arrive(NB, q_sum)
    total = s.q_recv[0]
    for k in range(1, NB):
        total += s.q_recv[k]
    s.qe[b] = total.astype(BF16)

    def q_all(d):
        return push(s.qe.at[b], s.qe.at[b], s.ss_e.at[d], s.rs_e.at[d], qry=at_b(d)[1])

    start(NB, q_all)
    loads[4].wait()
    arrive(NX, l_rows)
    arrive(NB, q_all)

    qe = s.qe[...].reshape(here, width)
    s.t_part[...] = dot(qe, s.lp[...], COLS).reshape(NLAB, quart, d_blk)

    def t_sum(d):
        nj = at_lab(d)
        return push(s.t_part.at[nj], s.t_recv.at[j], s.ss_t.at[d], s.rs_t.at[d], lab=nj)

    start(NLAB, t_sum)
    s.t_recv[j] = s.t_part[j]

    arrive(NLAB, count)
    counts = jnp.sum(s.c_recv[0] + s.c_recv[1] + s.c_recv[2] + s.c_recv[3], axis=0, keepdims=True)
    s.weight[...] = (1.0 - 0.99) / (1.0 - jnp.exp((counts + 1.0) * float(np.log(np.float64(np.float32(0.99))))))

    arrive(NLAB, t_sum)
    s.t_own[...] = (s.t_recv[0] + s.t_recv[1] + s.t_recv[2] + s.t_recv[3]).astype(BF16)
    t_swap = push(s.t_own, s.t_peer, s.ss_ty, s.rs_ty, qry=y_peer)
    t_swap.start()
    t_swap.wait_recv()

    @pl.when(y == 0)
    def _():
        s.t_pair[:, :d_blk] = s.t_own[...]
        s.t_pair[:, d_blk:] = s.t_peer[...]

    @pl.when(y == 1)
    def _():
        s.t_pair[:, :d_blk] = s.t_peer[...]
        s.t_pair[:, d_blk:] = s.t_own[...]

    s.t[x, 0, :, rows(z, d_pair)] = s.t_pair[:own, :]
    s.t[x, 1, :, rows(z, d_pair)] = s.t_pair[own:, :]

    def t_x(d):
        spot = s.t.at[x, 0, :, rows(z, d_pair)]
        return push(spot, spot, s.ss_t1.at[d], s.rs_t1.at[d], qry=at_x(d)[1])

    def t_z(d):
        spot = s.t.at[x, 1, :, rows(z, d_pair)]
        return push(spot, spot, s.ss_t2.at[d], s.rs_t2.at[d], qry=at_z(d)[1])

    def t_xz(d):
        spot = s.t.at[:, 0, :, rows(z, d_pair)]
        return push(spot, spot, s.ss_t3.at[d], s.rs_t3.at[d], qry=at_z(d)[1])

    def t_zx(d):
        spot = s.t.at[x, 1]
        return push(spot, spot, s.ss_t4.at[d], s.rs_t4.at[d], qry=at_x(d)[1])

    start(NX, t_x)
    start(NZ, t_z)
    arrive(NX, t_x)
    start(NZ, t_xz)
    arrive(NZ, t_z)
    start(NX, t_zx)
    loads[5].wait()
    arrive(NZ, t_xz)
    arrive(NX, t_zx)

    tall = 32

    def label_block(c, carry):
        cols = rows(c, wide)
        s.logit[...] = dot(s.t[...].reshape(here, NB * d_blk), s.lh[cols, :], COLS) * temper
        weight = s.weight[:, cols]

        def row_block(r, loss):
            at = rows(r, tall)
            value = s.logit[at, :]
            hit = s.mask[at, cols] > 0.0
            value = jnp.where(hit, -value, value)
            small = jnp.exp(-jnp.abs(value))
            soft = jnp.maximum(value, 0.0) + jnp.log1p(small)
            over = 1.0 / (1.0 + small)
            under = small * over
            high = value >= 0.0
            chance, rest = jnp.where(high, over, under), jnp.where(high, under, over)
            square = chance * chance
            slope = weight * (square * (chance + 2.0 * rest * soft)) * temper
            s.gl[at, cols] = jnp.where(hit, -slope, slope).astype(BF16)
            return loss + jnp.sum((weight * (square * soft)).reshape(tall // 8, 8, wide), axis=0)

        s.l_part[:, cols] = lax.fori_loop(0, here // tall, row_block, jnp.zeros((8, wide), F32))
        return carry

    lax.fori_loop(0, n_label // wide, label_block, 0)

    def u_z(d):
        nz, dev = at_z(d)
        return push(s.u_part.at[:, 0, :, rows(nz, d_pair)], s.u_rz.at[z], s.ss_u1.at[d], s.rs_u1.at[d], qry=dev)

    def u_x(d):
        nx, dev = at_x(d)
        return push(s.u_part.at[nx, 1], s.u_rx.at[x], s.ss_u2.at[d], s.rs_u2.at[d], qry=dev)

    def u_zx(d):
        nx, dev = at_x(d)
        return push(s.u_sz.at[nx], s.u_rzx.at[x], s.ss_u3.at[d], s.rs_u3.at[d], qry=dev)

    def u_xz(d):
        nz, dev = at_z(d)
        return push(s.u_sx.at[:, rows(nz, d_pair)], s.u_rxz.at[z], s.ss_u4.at[d], s.rs_u4.at[d], qry=dev)

    def u_block(d):
        cols = rows(lax.rem(z + d, NZ), d_pair)
        part = dot(s.gl[...], s.lh[:, cols])
        s.u_part[:, :, :, cols] = part.astype(BF16).reshape(NX, 2, own, d_pair)

    def u_turn(d):
        u_block(d)
        u_z(d).start()

    each(NZ, u_turn)
    sent.append((NZ, u_z))
    u_block(0)
    start(NX, u_x)
    def loss_sum(d):
        return push(s.l_part, s.l_recv.at[j], s.ss_l.at[d], s.rs_l.at[d], lab=at_lab(d))

    start(NLAB, loss_sum)
    s.l_recv[j] = s.l_part[...]
    arrive(NZ, u_z)
    half = s.u_part[:, 0, :, rows(z, d_pair)].astype(F32)
    for d in range(1, NZ):
        half += s.u_rz[lax.rem(z + d, NZ)].astype(F32)
    s.u_sz[...] = half.astype(BF16)
    start(NX, u_zx)
    arrive(NX, u_x)
    half = s.u_part[x, 1].astype(F32)
    for d in range(1, NX):
        half += s.u_rx[lax.rem(x + d, NX)].astype(F32)
    s.u_sx[...] = half.astype(BF16)
    start(NZ, u_xz)
    arrive(NX, u_zx)
    half = s.u_sz[x].astype(F32)
    for d in range(1, NX):
        half += s.u_rzx[lax.rem(x + d, NX)].astype(F32)
    s.back[:own, :] = half
    arrive(NZ, u_xz)
    half = s.u_sx[:, rows(z, d_pair)].astype(F32)
    for d in range(1, NZ):
        half += s.u_rxz[lax.rem(z + d, NZ)].astype(F32)
    s.back[own:, :] = half
    back = s.back[...]

    @pl.when(y == 0)
    def _():
        s.u_keep[...] = back[:, :d_blk]
        s.u_give[...] = back[:, d_blk:]

    @pl.when(y == 1)
    def _():
        s.u_keep[...] = back[:, d_blk:]
        s.u_give[...] = back[:, :d_blk]

    u_swap = push(s.u_give, s.u_peer, s.ss_uy, s.rs_uy, qry=y_peer)
    u_swap.start()
    u_swap.wait_recv()
    s.u[j] = (s.u_keep[...] + s.u_peer[...]).astype(BF16)

    def u_all(d):
        return push(s.u.at[j], s.u.at[j], s.ss_v.at[d], s.rs_v.at[d], lab=at_lab(d))

    start(NLAB, u_all)
    arrive(NLAB, u_all)
    u = s.u[...].reshape(here, d_blk)

    part = dot(u, s.lp[...]).reshape(NB, own, width)
    s.g_part[...] = part
    s.g_send[...] = part.astype(BF16)

    def g_sum(d):
        nb, dev = at_b(d)
        return push(s.g_send.at[nb], s.g_recv.at[b], s.ss_g.at[d], s.rs_g.at[d], qry=dev)

    start(NB, g_sum)
    part = dot(u, qe, ROWS).reshape(NX, d_row, width)
    s.k_part[...] = part
    s.k_send[...] = part.astype(BF16)

    def k_sum(d):
        nx, dev = at_x(d)
        return push(s.k_send.at[nx], s.k_recv.at[x], s.ss_k.at[d], s.rs_k.at[d], qry=dev)

    start(NX, k_sum)
    arrive(NB, g_sum)
    total = s.g_part[b]
    for d in range(1, NB):
        total += s.g_recv[lax.rem(b + d, NB)].astype(F32)
    gqe_out[...] = total
    s.ge[b] = total.astype(BF16)

    def g_all(d):
        return push(s.ge.at[b], s.ge.at[b], s.ss_h.at[d], s.rs_h.at[d], qry=at_b(d)[1])

    start(NB, g_all)
    arrive(NLAB, loss_sum)
    losses = jnp.sum(s.l_recv[0] + s.l_recv[1] + s.l_recv[2] + s.l_recv[3], axis=0, keepdims=True)
    loss_out[...] = losses / n_query
    arrive(NX, k_sum)
    total = s.k_part[x]
    for d in range(1, NX):
        total += s.k_recv[lax.rem(x + d, NX)].astype(F32)
    glp_out[...] = total

    arrive(NB, g_all)
    part = dot(s.q_blk[...].reshape(here, e_blk), s.ge[...].reshape(here, width), ROWS).reshape(NX, e_row, width)
    s.p_part[...] = part
    s.p_send[...] = part.astype(BF16)

    def p_sum(d):
        nx, dev = at_x(d)
        return push(s.p_send.at[nx], s.p_recv.at[x], s.ss_q.at[d], s.rs_q.at[d], qry=dev)

    start(NX, p_sum)
    arrive(NX, p_sum)
    total = s.p_part[x]
    for d in range(1, NX):
        total += s.p_recv[lax.rem(x + d, NX)].astype(F32)
    gqp_out[...] = total

    for number, copies in sent:
        each(number, lambda d: copies(d).wait_send())
    t_swap.wait_send()
    u_swap.wait_send()
    ids_sent()


class Scratch:
    def __init__(self, names, refs):
        for name, ref in zip(names, refs):
            setattr(self, name, ref)


def shards(query_hidden, query_proj, label_hidden, label_proj, pos_ids, pos_count):
    own, wide_e = query_hidden.shape
    n_label, wide_d = label_hidden.shape
    e_row, width = query_proj.shape
    d_row = label_proj.shape[0]
    slots = pos_ids.shape[1]
    e_blk, d_blk = wide_e // NB, wide_d // NB
    here, quart = NB * own, NB * own // NLAB
    vmem, dma = pltpu.VMEM, pltpu.SemaphoreType.DMA
    scratch = {
        "lh": vmem((n_label, wide_d), BF16),
        "q_send": vmem((NB, own, e_blk), BF16),
        "q_blk": vmem((NB, own, e_blk), BF16),
        "qp": vmem((NX * e_row, width), BF16),
        "lp": vmem((NX * d_row, width), BF16),
        "qh": vmem((own, wide_e), BF16),
        "ids_raw": vmem((slots, own), jnp.int32),
        "used": vmem((1, own), jnp.int32),
        "ids_send": vmem((slots, 128), jnp.int32),
        "ids": vmem((NB, slots, 128), jnp.int32),
        "mask": vmem((here, n_label), F32),
        "c_part": vmem((8, n_label), F32),
        "c_recv": vmem((NLAB, 8, n_label), F32),
        "weight": vmem((1, n_label), F32),
        "q_part": vmem((NB, own, width), F32),
        "q_recv": vmem((NB, own, width), F32),
        "qe": vmem((NB, own, width), BF16),
        "t_part": vmem((NLAB, quart, d_blk), F32),
        "t_recv": vmem((NLAB, quart, d_blk), F32),
        "t_own": vmem((quart, d_blk), BF16),
        "t_peer": vmem((quart, d_blk), BF16),
        "t_pair": vmem((quart, 2 * d_blk), BF16),
        "t": vmem((NX, 2, own, wide_d), BF16),
        "logit": vmem((here, 256), F32),
        "gl": vmem((here, n_label), BF16),
        "l_part": vmem((8, n_label), F32),
        "l_recv": vmem((NLAB, 8, n_label), F32),
        "u_part": vmem((NX, 2, own, wide_d), BF16),
        "u_rz": vmem((NZ, NX, own, 2 * d_blk), BF16),
        "u_rx": vmem((NX, own, wide_d), BF16),
        "u_sz": vmem((NX, own, 2 * d_blk), BF16),
        "u_sx": vmem((own, wide_d), BF16),
        "u_rzx": vmem((NX, own, 2 * d_blk), BF16),
        "u_rxz": vmem((NZ, own, 2 * d_blk), BF16),
        "back": vmem((quart, 2 * d_blk), F32),
        "u_keep": vmem((quart, d_blk), F32),
        "u_give": vmem((quart, d_blk), F32),
        "u_peer": vmem((quart, d_blk), F32),
        "u": vmem((NLAB, quart, d_blk), BF16),
        "g_part": vmem((NB, own, width), F32),
        "g_send": vmem((NB, own, width), BF16),
        "g_recv": vmem((NB, own, width), BF16),
        "ge": vmem((NB, own, width), BF16),
        "k_part": vmem((NX, d_row, width), F32),
        "k_send": vmem((NX, d_row, width), BF16),
        "k_recv": vmem((NX, d_row, width), BF16),
        "p_part": vmem((NX, e_row, width), F32),
        "p_send": vmem((NX, e_row, width), BF16),
        "p_recv": vmem((NX, e_row, width), BF16),
        "load": dma((6,)),
    }
    for name, count in (
        ("a", NB), ("w", NX), ("d", NX), ("b", NB), ("e", NB), ("c", NLAB), ("t", NLAB), ("t1", NX), ("t2", NZ), ("t3", NZ), ("t4", NX),
        ("u1", NZ), ("u2", NX), ("u3", NX), ("u4", NZ),
        ("v", NLAB), ("l", NLAB), ("g", NB), ("h", NB), ("k", NX), ("q", NX),
    ):
        scratch["ss_" + name] = dma((count,))
        scratch["rs_" + name] = dma((count,))
    scratch["ss_i"], scratch["rs_i"] = dma((NX * NZ,)), dma((NX,))
    for name in ("ss_ty", "rs_ty", "ss_uy", "rs_uy", "ss_iy", "rs_iy"):
        scratch[name] = dma(())
    names = tuple(scratch)
    in_vmem = pl.BlockSpec(memory_space=pltpu.VMEM)

    def kernel(*refs):
        step_kernel(wide_e ** (-0.5), NQRY * own, *refs[:10], Scratch(names, refs[10:]))

    arrays = [
        pltpu.with_memory_space_constraint(a, pltpu.HBM)
        for a in (query_hidden, query_proj, label_hidden, label_proj, pos_ids.T, pos_count.reshape(1, own))
    ]
    gqp, glp, loss, gqe = pl.pallas_call(
        kernel,
        out_shape=(
            jax.ShapeDtypeStruct((e_row, width), F32),
            jax.ShapeDtypeStruct((d_row, width), F32),
            jax.ShapeDtypeStruct((1, n_label), F32),
            jax.ShapeDtypeStruct((own, width), F32),
        ),
        in_specs=[pl.BlockSpec(memory_space=pltpu.HBM)] * 6,
        out_specs=(in_vmem,) * 4,
        scratch_shapes=list(scratch.values()),
        compiler_params=pltpu.CompilerParams(
            collective_id=0, has_side_effects=True, vmem_limit_bytes=48 << 20
        ),
        name="focal_step",
    )(*arrays)
    return gqp, glp, loss.reshape(n_label), gqe


def solution(mesh):
    in_specs = (
        P("qry", None),
        P("qry", "lab"),
        P("qry", None),
        P("qry", "lab"),
        P("qry", None),
        P("qry"),
    )
    out_specs = (P("qry", "lab"), P("qry", "lab"), P("qry"), P("qry", "lab"))
    return jax.shard_map(shards, mesh=mesh, in_specs=in_specs, out_specs=out_specs, check_vma=False)
```

time: 122 us -> 110 us (0.902); the launches traced: 121 us -> 110 us
  local copies, waits for them, and re-layouts: 8.06 us -> 2.66 us
  Pallas kernels: 111 us -> 107 us
    unnamed x13 -> x4, local copies, waits for them, and re-layouts: 8.06 us -> 2.66 us
    pallas_call x1, Pallas kernels: 111 us -> 107 us  [shards(): pl.pallas_call(kernel, out_shape=(jax.ShapeDtypeStruct((e_row, width), F3...]
where the time goes in v2:
time: 110 us
  Pallas kernels  107 us (97%)
  local copies, waits for them, and re-layouts  2.66 us (2%)
    pallas_call x1, Pallas kernels, shards(): pl.pallas_call(kernel, out_shape=(jax.ShapeDtypeStruct((e_row, width), F3...  107 us
    unnamed x4, local copies, waits for them, and re-layouts  2.66 us

profile of v2, /device:TPU:0, one launch (start us, length us, event | category | flops | bytes accessed | tf_op | source)
XLA Modules:
  0.0 110.3 jit_solution(410601330699163240)
XLA Ops:
  0.6 107.0 %focal_step.1 = (f32[112,896]{1,0:T(8,128)S(1)}, f32[48,896]{1,0:T(8,128)S(1)}, f32[1,1024]{1,0:T(1,128)S(1)}, f32[32,896]{1,0:T(8,128)S(1)}) custom-call(bf16[32,3584]{1,0:T(8,128)(2,1)} %refs_0_.1, bf16[112,896]{1,0:T(8,128)(2,1)} %refs_1_.1, bf16[1024,1536]{1,0:T(8,128)(2,1)} %refs_2_.1, bf16[48,896]{1,0:T(8,128)(2,1)} %refs_3_.1, s32[8,32]{1,0:T(8,128)} %bitcast.4, ...), custom_call_target="tpu_custom_call" | custom-call | tf_op jit(solution)/shard_map/focal_step/pallas_call | solution.py:517
  107.6 0.8 copy.14
  108.3 0.7 copy.15
  109.0 0.6 copy.16
  109.6 0.6 copy.17

commit v3 on v0

v3 whole, which is shorter than its diff:
```python
import jax
import jax.numpy as jnp
import numpy as np
from jax import lax
from jax.experimental import pallas as pl
from jax.experimental.pallas import tpu as pltpu
from jax.sharding import PartitionSpec as P

NX, NY, NZ, NLAB = 4, 2, 4, 4
NQRY = NX * NY * NZ
ROWS = (((0,), (0,)), ((), ()))
COLS = (((1,), (1,)), ((), ()))
MESH = pl.DeviceIdType.MESH
F32, BF16 = jnp.float32, jnp.bfloat16


def dot(left, right, dims=(((1,), (0,)), ((), ()))):
    return lax.dot_general(left, right, dims, preferred_element_type=F32)


def each(count, step):
    def body(d, carry):
        step(d)
        return carry

    lax.fori_loop(1, count, body, 0)


def step_kernel(temper, cut, qh, qp, lh, lp, ids, used, gqp_out, glp_out, loss_out, gqe_out, s):
    own = qh.shape[0]
    e_row, d_row, width = qp.shape[0], lp.shape[0], qp.shape[1]
    n_label, wide_d = lh.shape
    e_z, d_z = NX * NY * e_row, NX * NY * d_row
    e_b = NX * e_row
    here, block = NX * NY * own, NZ * own
    me, j = lax.axis_index("qry"), lax.axis_index("lab")
    x, y, z = lax.rem(me, NX), lax.rem(lax.div(me, NX), NY), lax.div(me, NX * NY)

    def at(nz, ny, nx):
        return {"qry": (nz * NY + ny) * NX + nx}

    y_peer = at(z, 1 - y, x)

    def next_x(d):
        return lax.rem(x + d, NX)

    def next_z(d):
        return lax.rem(z + d, NZ)

    def next_lab(d):
        return lax.rem(j + d, NLAB)

    def rows(index, size):
        return pl.ds(pl.multiple_of(index * size, size), size)

    def push(name, d, src, dst, device):
        return pltpu.make_async_remote_copy(
            src_ref=src,
            dst_ref=dst,
            send_sem=getattr(s, "send_" + name).at[d],
            recv_sem=getattr(s, "recv_" + name).at[d],
            device_id=device,
            device_id_type=MESH,
        )

    sent = []

    def start(count, copies):
        each(count, lambda d: copies(d).start())
        sent.append((count, copies))

    def arrive(count, copies):
        each(count, lambda d: copies(d).wait_recv())

    loads = [
        pltpu.make_async_copy(source, target, s.load.at[k])
        for k, (source, target) in enumerate(
            (
                (qh, s.qh),
                (ids, s.ids_raw),
                (used, s.used),
                (qp.at[:, pl.ds(0, cut)], s.wx.at[y, x]),
                (qp.at[:, pl.ds(cut, width - cut)], s.wz.at[z, y]),
                (lp, s.lp.at[y, x]),
                (lh, s.lh),
            )
        )
    ]
    for load in loads:
        load.start()

    barrier = pltpu.get_barrier_semaphore()

    def greet(device):
        pl.semaphore_signal(barrier, inc=1, device_id=device, device_id_type=MESH)

    each(NX, lambda d: greet(at(z, y, next_x(d))))
    each(NZ, lambda d: greet(at(next_z(d), y, x)))
    greet(y_peer)
    each(NX, lambda d: greet(at(z, 1 - y, next_x(d))))
    each(NZ, lambda d: greet(at(next_z(d), 1 - y, x)))
    each(NLAB, lambda d: greet({"lab": next_lab(d)}))

    loads[0].wait()
    for k in range(NX):
        s.q1_send[k] = jnp.concatenate(
            [s.qh[:, (NX * r + k) * e_row : (NX * r + k + 1) * e_row] for r in range(NZ * NY)], axis=1
        )
    for k in range(NZ * NY):
        s.qx_send[k] = s.qh[:, k * e_b : (k + 1) * e_b]
    for nx in range(NX):
        for ny in range(NY):
            first = [(NX * (NY * r + ny) + nx) * e_row for r in range(NZ)]
            s.qz_send[NY * nx + ny] = jnp.concatenate([s.qh[:, f : f + e_row] for f in first], axis=1)
    loads[1].wait()
    loads[2].wait()
    slots = ids.shape[0]
    s.ids_send[...] = jnp.full(s.ids_send.shape, -1, jnp.int32)
    slot_at = lax.broadcasted_iota(jnp.int32, ids.shape, 0)
    s.ids_send[:, :own] = jnp.where(slot_at < s.used[...], s.ids_raw[...], -1)
    pl.semaphore_wait(barrier, 2 * (NX - 1) + 2 * (NZ - 1) + 1 + NLAB - 1)

    x_cols, z_cols = pl.ds(0, cut), pl.ds(cut, width - cut)

    def w_yx(d):
        return push("w_yx", d, qp.at[:, x_cols], s.wx.at[y, x], y_peer)

    def w_yz(d):
        return push("w_yz", d, qp.at[:, z_cols], s.wz.at[z, y], y_peer)

    def w_x(d):
        return push("w_x", d, qp.at[:, x_cols], s.wx.at[y, x], at(z, y, next_x(d)))

    def w_z(d):
        return push("w_z", d, qp.at[:, z_cols], s.wz.at[z, y], at(next_z(d), y, x))

    def w_fx(d):
        return push("w_fx", d, s.wx.at[1 - y, x], s.wx.at[1 - y, x], at(z, y, next_x(d)))

    def w_fz(d):
        return push("w_fz", d, s.wz.at[z, 1 - y], s.wz.at[z, 1 - y], at(next_z(d), y, x))

    def q0(d):
        return push("q0", d, qh.at[:, rows(next_z(d), e_z)], s.q0.at[z], at(next_z(d), y, x))

    def q1(d):
        return push("q1", d, s.q1_send.at[next_x(d)], s.q1.at[x], at(z, y, next_x(d)))

    def l_x(d):
        return push("l_x", d, lp, s.lp.at[y, x], at(z, y, next_x(d)))

    def l_y(d):
        return push("l_y", d, s.lp.at[y], s.lp.at[y], y_peer)

    start(2, w_yx)
    start(2, w_yz)
    start(NX, w_x)
    start(NZ, w_z)
    start(NZ, q0)
    start(NX, q1)
    start(NX, l_x)

    def i_y(d):
        return push("i_y", d, s.ids_send, s.ids.at[x, y], y_peer)

    def i_x(d):
        return push("i_x", d, s.ids.at[x], s.ids.at[x], at(z, y, next_x(d)))

    def i_z(d):
        return push("i_z", d, s.ids, s.ids, at(next_z(d), y, x))

    holder = z == j

    @pl.when(holder)
    def _():
        i_y(1).start()
        s.ids[x, y] = s.ids_send[...]
        i_y(1).wait_recv()
        each(NX, lambda d: i_x(d).start())

    s.q0[z] = s.qh[:, rows(z, e_z)]
    s.q1[x] = s.q1_send[x]
    arrive(2, w_yx)
    start(NX, w_fx)
    arrive(2, w_yz)
    start(NZ, w_fz)

    @pl.when(holder)
    def _():
        arrive(NX, i_x)
        each(NZ, lambda d: i_z(d).start())

    def ids_arrive():
        @pl.when(jnp.logical_not(holder))
        def _():
            i_z(lax.rem(z - j + NZ, NZ)).wait_recv()

    def ids_sent():
        @pl.when(holder)
        def _():
            i_y(1).wait_send()
            each(NX, lambda d: i_x(d).wait_send())
            each(NZ, lambda d: i_z(d).wait_send())

    arrive(NX, l_x)
    loads[5].wait()
    start(2, l_y)

    arrive(NZ, q0)
    arrive(NX, w_x)
    loads[3].wait()
    arrive(NX, w_fx)
    s.part_z[...] = dot(s.q0[...].reshape(block, e_z), s.wx[...].reshape(e_z, cut)).reshape(NZ, own, cut)

    def b_z(d):
        return push("b_z", d, s.part_z.at[next_z(d)], s.sum_z.at[z], at(next_z(d), y, x))

    start(NZ, b_z)
    arrive(NX, q1)
    arrive(NZ, w_z)
    loads[4].wait()
    arrive(NZ, w_fz)
    s.part_x[...] = dot(s.q1[...].reshape(block, e_z), s.wz[...].reshape(e_z, width - cut)).reshape(NX, own, width - cut)

    def b_x(d):
        return push("b_x", d, s.part_x.at[next_x(d)], s.sum_x.at[x], at(z, y, next_x(d)))

    start(NX, b_x)
    s.sum_z[z] = s.part_z[z]
    s.sum_x[x] = s.part_x[x]

    ids_arrive()
    local = s.ids[...].reshape(NX * NY * slots, s.ids.shape[3]).T - n_label * me
    wide = 256
    for c in range(n_label // wide):
        column = lax.broadcasted_iota(jnp.int32, (own, wide), 1) + c * wide
        tally = jnp.zeros((8, wide), F32)
        for k in range(NX * NY):
            found = jnp.zeros((own, wide), F32)
            for slot in range(k * slots, (k + 1) * slots):
                found += jnp.where(local[:own, slot : slot + 1] == column, 1.0, 0.0)
            s.mask[k * own : (k + 1) * own, c * wide : (c + 1) * wide] = found
            tally += jnp.sum(found.reshape(own // 8, 8, wide), axis=0)
        s.c_part[:, c * wide : (c + 1) * wide] = tally

    def count(d):
        return push("count", d, s.c_part, s.c_recv.at[j], {"lab": next_lab(d)})

    start(NLAB, count)
    s.c_recv[j] = s.c_part[...]

    arrive(NZ, b_z)
    s.qe[z, :, :cut] = (s.sum_z[0] + s.sum_z[1] + s.sum_z[2] + s.sum_z[3]).astype(BF16)
    arrive(NX, b_x)
    s.qe[z, :, cut:] = (s.sum_x[0] + s.sum_x[1] + s.sum_x[2] + s.sum_x[3]).astype(BF16)

    def q_all(d):
        return push("q_all", d, s.qe.at[z], s.qe.at[z], at(next_z(d), y, x))

    start(NZ, q_all)
    arrive(2, l_y)
    arrive(NZ, q_all)

    s.t_part[...] = dot(s.qe[...].reshape(block, width), s.lp[...].reshape(d_z, width), COLS).reshape(NLAB, own, d_z)

    def t_sum(d):
        return push("t_sum", d, s.t_part.at[next_lab(d)], s.t_recv.at[j], {"lab": next_lab(d)})

    start(NLAB, t_sum)
    s.t_recv[j] = s.t_part[j]

    arrive(NLAB, count)
    counts = jnp.sum(s.c_recv[0] + s.c_recv[1] + s.c_recv[2] + s.c_recv[3], axis=0, keepdims=True)
    s.weight[...] = (1.0 - 0.99) / (1.0 - jnp.exp((counts + 1.0) * float(np.log(np.float64(np.float32(0.99))))))

    arrive(NLAB, t_sum)
    mine = rows(z, d_z)
    s.t[x, y, :, mine] = (s.t_recv[0] + s.t_recv[1] + s.t_recv[2] + s.t_recv[3]).astype(BF16)

    def t_y(d):
        return push("t_y", d, s.t.at[x, y, :, mine], s.t.at[x, y, :, mine], y_peer)

    def t_x(d):
        return push("t_x", d, s.t.at[x, 0, :, mine], s.t.at[x, 0, :, mine], at(z, y, next_x(d)))

    def t_z(d):
        return push("t_z", d, s.t.at[x, 1, :, mine], s.t.at[x, 1, :, mine], at(next_z(d), y, x))

    def t_xz(d):
        return push("t_xz", d, s.t.at[:, 0, :, mine], s.t.at[:, 0, :, mine], at(next_z(d), y, x))

    def t_zx(d):
        return push("t_zx", d, s.t.at[x, 1], s.t.at[x, 1], at(z, y, next_x(d)))

    start(2, t_y)
    arrive(2, t_y)
    start(NX, t_x)
    start(NZ, t_z)
    arrive(NX, t_x)
    start(NZ, t_xz)
    arrive(NZ, t_z)
    start(NX, t_zx)
    loads[6].wait()
    arrive(NZ, t_xz)
    arrive(NX, t_zx)

    def in_b(d):
        return lax.rem(z + lax.div(d, NY), NZ), lax.rem(y + lax.rem(d, NY), NY)

    def in_c(d):
        return lax.rem(x + lax.div(d, NY), NX), lax.rem(y + lax.rem(d, NY), NY)

    spot_b, spot_c = NY * z + y, NY * x + y

    def q_bx(d):
        nz, ny = in_b(d)
        return push("q_bx", d, s.qx_send.at[NY * nz + ny], s.qx.at[spot_b], at(nz, ny, x))

    def q_bz(d):
        nx, ny = in_c(d)
        return push("q_bz", d, s.qz_send.at[NY * nx + ny], s.qz.at[spot_c], at(z, ny, nx))

    start(NZ * NY, q_bx)
    start(NX * NY, q_bz)
    s.qx[spot_b] = s.qx_send[spot_b]
    s.qz[spot_c] = s.qz_send[spot_c]

    tall = 32

    def label_block(c, carry):
        cols = rows(c, wide)
        s.logit[...] = dot(s.t[...].reshape(here, wide_d), s.lh[cols, :], COLS) * temper
        weight = s.weight[:, cols]

        def row_block(r, loss):
            some = rows(r, tall)
            value = s.logit[some, :]
            hit = s.mask[some, cols] > 0.0
            value = jnp.where(hit, -value, value)
            small = jnp.exp(-jnp.abs(value))
            soft = jnp.maximum(value, 0.0) + jnp.log1p(small)
            over = 1.0 / (1.0 + small)
            under = small * over
            high = value >= 0.0
            chance, rest = jnp.where(high, over, under), jnp.where(high, under, over)
            square = chance * chance
            slope = weight * (square * (chance + 2.0 * rest * soft)) * temper
            s.gl[some, cols] = jnp.where(hit, -slope, slope).astype(BF16)
            return loss + jnp.sum((weight * (square * soft)).reshape(tall // 8, 8, wide), axis=0)

        s.l_part[:, cols] = lax.fori_loop(0, here // tall, row_block, jnp.zeros((8, wide), F32))
        return carry

    lax.fori_loop(0, n_label // wide, label_block, 0)

    def u_z(d):
        return push("u_z", d, s.u_part.at[:, 0, :, rows(next_z(d), d_z)], s.u_rz.at[z], at(next_z(d), y, x))

    def u_x(d):
        return push("u_x", d, s.u_part.at[next_x(d), 1], s.u_rx.at[x], at(z, y, next_x(d)))

    def u_zx(d):
        return push("u_zx", d, s.u_sz.at[next_x(d)], s.u_rzx.at[x], at(z, y, next_x(d)))

    def u_xz(d):
        return push("u_xz", d, s.u_sx.at[:, rows(next_z(d), d_z)], s.u_rxz.at[z], at(next_z(d), y, x))

    def u_block(d):
        cols = rows(next_z(d), d_z)
        part = dot(s.gl[...], s.lh[:, cols])
        s.u_part[:, :, :, cols] = part.astype(BF16).reshape(NX, NY, own, d_z)

    def u_turn(d):
        u_block(d)
        u_z(d).start()

    each(NZ, u_turn)
    sent.append((NZ, u_z))
    u_block(0)
    start(NX, u_x)

    def loss_sum(d):
        return push("loss", d, s.l_part, s.l_recv.at[j], {"lab": next_lab(d)})

    start(NLAB, loss_sum)
    s.l_recv[j] = s.l_part[...]
    arrive(NZ, u_z)
    half = s.u_part[:, 0, :, mine].astype(F32)
    for d in range(1, NZ):
        half += s.u_rz[next_z(d)].astype(F32)
    s.u_sz[...] = half.astype(BF16)
    start(NX, u_zx)
    arrive(NX, u_x)
    half = s.u_part[x, 1].astype(F32)
    for d in range(1, NX):
        half += s.u_rx[next_x(d)].astype(F32)
    s.u_sx[...] = half.astype(BF16)
    start(NZ, u_xz)
    arrive(NX, u_zx)
    half = s.u_sz[x].astype(F32)
    for d in range(1, NX):
        half += s.u_rzx[next_x(d)].astype(F32)
    s.back[0] = half
    arrive(NZ, u_xz)
    half = s.u_sx[:, mine].astype(F32)
    for d in range(1, NZ):
        half += s.u_rxz[next_z(d)].astype(F32)
    s.back[1] = half

    def u_y(d):
        return push("u_y", d, s.back.at[1 - y], s.u_peer, y_peer)

    start(2, u_y)
    arrive(2, u_y)
    s.u[j] = (s.back[y] + s.u_peer[...]).astype(BF16)

    def u_all(d):
        return push("u_all", d, s.u.at[j], s.u.at[j], {"lab": next_lab(d)})

    start(NLAB, u_all)
    arrive(NLAB, u_all)
    u = s.u[...].reshape(block, d_z)

    part = dot(u, s.lp[...].reshape(d_z, width)).reshape(NZ, own, width)
    s.g_part[...] = part
    s.g_send[...] = part.astype(BF16)

    def g_sum(d):
        return push("g_sum", d, s.g_send.at[next_z(d)], s.g_recv.at[z], at(next_z(d), y, x))

    start(NZ, g_sum)
    part = dot(u, s.qe[...].reshape(block, width), ROWS).reshape(NY, NX, d_row, width)
    s.k_part[...] = part
    s.k_send[...] = part.astype(BF16)

    def k_x(d):
        return push("k_x", d, s.k_send.at[:, next_x(d)], s.k_recv.at[x], at(z, y, next_x(d)))

    start(NX, k_x)
    arrive(NZ, g_sum)
    total = s.g_part[z]
    for d in range(1, NZ):
        total += s.g_recv[next_z(d)].astype(F32)
    gqe_out[...] = total
    s.ge[...] = total.astype(BF16)

    def g_bx(d):
        nz, ny = in_b(d)
        return push("g_bx", d, s.ge.at[:, x_cols], s.gx.at[spot_b], at(nz, ny, x))

    def g_bz(d):
        nx, ny = in_c(d)
        return push("g_bz", d, s.ge.at[:, z_cols], s.gz.at[spot_c], at(z, ny, nx))

    start(NZ * NY, g_bx)
    start(NX * NY, g_bz)
    s.gx[spot_b] = s.ge[:, :cut]
    s.gz[spot_c] = s.ge[:, cut:]
    arrive(NLAB, loss_sum)
    losses = jnp.sum(s.l_recv[0] + s.l_recv[1] + s.l_recv[2] + s.l_recv[3], axis=0, keepdims=True)
    loss_out[...] = losses / (NQRY * own)
    arrive(NZ * NY, q_bx)
    arrive(NX * NY, q_bz)

    arrive(NZ * NY, g_bx)
    part = dot(s.qx[...].reshape(here, e_b), s.gx[...].reshape(here, cut), ROWS).reshape(NX, e_row, cut)
    s.px_part[...] = part
    s.px_send[...] = part.astype(BF16)

    def p_x(d):
        return push("p_x", d, s.px_send.at[next_x(d)], s.px_recv.at[x], at(z, y, next_x(d)))

    start(NX, p_x)
    arrive(NX * NY, g_bz)
    part = dot(s.qz[...].reshape(here, e_b), s.gz[...].reshape(here, width - cut), ROWS).reshape(NZ, e_row, width - cut)
    s.pz_part[...] = part
    s.pz_send[...] = part.astype(BF16)

    def p_z(d):
        return push("p_z", d, s.pz_send.at[next_z(d)], s.pz_recv.at[z], at(next_z(d), y, x))

    start(NZ, p_z)

    arrive(NX, k_x)
    total = s.k_part[:, x]
    for d in range(1, NX):
        total += s.k_recv[next_x(d)].astype(F32)
    s.k_sum[...] = total

    def k_y(d):
        return push("k_y", d, s.k_sum.at[1 - y], s.k_peer, y_peer)

    start(2, k_y)
    arrive(NX, p_x)
    total = s.px_part[x]
    for d in range(1, NX):
        total += s.px_recv[next_x(d)].astype(F32)
    gqp_out[:, :cut] = total
    arrive(2, k_y)
    glp_out[...] = s.k_sum[y] + s.k_peer[...]
    arrive(NZ, p_z)
    total = s.pz_part[z]
    for d in range(1, NZ):
        total += s.pz_recv[next_z(d)].astype(F32)
    gqp_out[:, cut:] = total

    for number, copies in sent:
        each(number, lambda d: copies(d).wait_send())
    ids_sent()


class Scratch:
    def __init__(self, names, refs):
        for name, ref in zip(names, refs):
            setattr(self, name, ref)


def shards(query_hidden, query_proj, label_hidden, label_proj, pos_ids, pos_count):
    own, wide_e = query_hidden.shape
    n_label, wide_d = label_hidden.shape
    e_row, width = query_proj.shape
    d_row = label_proj.shape[0]
    slots = pos_ids.shape[1]
    e_z, d_z, e_b = NX * NY * e_row, NX * NY * d_row, NX * e_row
    here = NX * NY * own
    cut = width // 256 * 128
    rest = width - cut
    scratch = {
        "qh": ((own, wide_e), BF16),
        "ids_raw": ((slots, own), jnp.int32),
        "used": ((1, own), jnp.int32),
        "ids_send": ((slots, 128), jnp.int32),
        "ids": ((NX, NY, slots, 128), jnp.int32),
        "lh": ((n_label, wide_d), BF16),
        "lp": ((NY, NX, d_row, width), BF16),
        "wx": ((NY, NX, e_row, cut), BF16),
        "wz": ((NZ, NY, e_row, rest), BF16),
        "q0": ((NZ, own, e_z), BF16),
        "q1_send": ((NX, own, e_z), BF16),
        "q1": ((NX, own, e_z), BF16),
        "qx_send": ((NZ * NY, own, e_b), BF16),
        "qx": ((NZ * NY, own, e_b), BF16),
        "qz_send": ((NX * NY, own, e_b), BF16),
        "qz": ((NX * NY, own, e_b), BF16),
        "part_z": ((NZ, own, cut), F32),
        "sum_z": ((NZ, own, cut), F32),
        "part_x": ((NX, own, rest), F32),
        "sum_x": ((NX, own, rest), F32),
        "mask": ((here, n_label), F32),
        "c_part": ((8, n_label), F32),
        "c_recv": ((NLAB, 8, n_label), F32),
        "weight": ((1, n_label), F32),
        "qe": ((NZ, own, width), BF16),
        "t_part": ((NLAB, own, d_z), F32),
        "t_recv": ((NLAB, own, d_z), F32),
        "t": ((NX, NY, own, wide_d), BF16),
        "logit": ((here, 256), F32),
        "gl": ((here, n_label), BF16),
        "l_part": ((8, n_label), F32),
        "l_recv": ((NLAB, 8, n_label), F32),
        "u_part": ((NX, NY, own, wide_d), BF16),
        "u_rz": ((NZ, NX, own, d_z), BF16),
        "u_rx": ((NX, own, wide_d), BF16),
        "u_sz": ((NX, own, d_z), BF16),
        "u_sx": ((own, wide_d), BF16),
        "u_rzx": ((NX, own, d_z), BF16),
        "u_rxz": ((NZ, own, d_z), BF16),
        "back": ((NY, own, d_z), F32),
        "u_peer": ((own, d_z), F32),
        "u": ((NLAB, own, d_z), BF16),
        "g_part": ((NZ, own, width), F32),
        "g_send": ((NZ, own, width), BF16),
        "g_recv": ((NZ, own, width), BF16),
        "ge": ((own, width), BF16),
        "gx": ((NZ * NY, own, cut), BF16),
        "gz": ((NX * NY, own, rest), BF16),
        "k_part": ((NY, NX, d_row, width), F32),
        "k_send": ((NY, NX, d_row, width), BF16),
        "k_recv": ((NX, NY, d_row, width), BF16),
        "k_sum": ((NY, d_row, width), F32),
        "k_peer": ((d_row, width), F32),
        "px_part": ((NX, e_row, cut), F32),
        "px_send": ((NX, e_row, cut), BF16),
        "px_recv": ((NX, e_row, cut), BF16),
        "pz_part": ((NZ, e_row, rest), F32),
        "pz_send": ((NZ, e_row, rest), BF16),
        "pz_recv": ((NZ, e_row, rest), BF16),
    }
    scratch = {name: pltpu.VMEM(*spec) for name, spec in scratch.items()}
    scratch["load"] = pltpu.SemaphoreType.DMA((7,))
    pairs = ("w_yx", "w_yz", "l_y", "i_y", "t_y", "u_y", "k_y")
    fours = (
        "w_x", "w_z", "w_fx", "w_fz", "q0", "q1", "l_x", "i_x", "i_z", "b_z", "b_x", "count", "q_all", "t_sum",
        "t_x", "t_z", "t_xz", "t_zx", "u_z", "u_x", "u_zx", "u_xz", "loss", "u_all", "g_sum", "k_x", "p_x", "p_z",
    )
    eights = ("q_bx", "q_bz", "g_bx", "g_bz")
    for number, group in ((2, pairs), (4, fours), (8, eights)):
        for name in group:
            scratch["send_" + name] = pltpu.SemaphoreType.DMA((number,))
            scratch["recv_" + name] = pltpu.SemaphoreType.DMA((number,))
    names = tuple(scratch)

    def kernel(*refs):
        step_kernel(wide_e ** (-0.5), cut, *refs[:10], Scratch(names, refs[10:]))

    arrays = [
        pltpu.with_memory_space_constraint(a, pltpu.HBM)
        for a in (query_hidden, query_proj, label_hidden, label_proj, pos_ids.T, pos_count.reshape(1, own))
    ]
    gqp, glp, loss, gqe = pl.pallas_call(
        kernel,
        out_shape=(
            jax.ShapeDtypeStruct((e_row, width), F32),
            jax.ShapeDtypeStruct((d_row, width), F32),
            jax.ShapeDtypeStruct((1, n_label), F32),
            jax.ShapeDtypeStruct((own, width), F32),
        ),
        in_specs=[pl.BlockSpec(memory_space=pltpu.HBM)] * 6,
        out_specs=(pl.BlockSpec(memory_space=pltpu.VMEM),) * 4,
        scratch_shapes=list(scratch.values()),
        compiler_params=pltpu.CompilerParams(
            collective_id=0, has_side_effects=True, vmem_limit_bytes=48 << 20
        ),
        name="focal_step",
    )(*arrays)
    return gqp, glp, loss.reshape(n_label), gqe


def solution(mesh):
    in_specs = (
        P("qry", None),
        P("qry", "lab"),
        P("qry", None),
        P("qry", "lab"),
        P("qry", None),
        P("qry"),
    )
    out_specs = (P("qry", "lab"), P("qry", "lab"), P("qry"), P("qry", "lab"))
    return jax.shard_map(shards, mesh=mesh, in_specs=in_specs, out_specs=out_specs, check_vma=False)
```

time: 1170 us -> 99.6 us (0.09)
  waiting for transfers between devices: 959 us -> 0 us
  Pallas kernels: 0 us -> 96.2 us
  blocking collectives: 94.9 us -> 0 us
  matrix products: 38.8 us -> 0 us
  other arithmetic: 35 us -> 0 us
  local copies, waits for them, and re-layouts: 24.2 us -> 2.66 us
  between operations: 14.9 us -> 0.64 us
    all_gather x3 -> x0, waiting for transfers between devices: 467 us -> none  [the longest x1 167 us: shards(): lax.all_gather(query_proj, 'qry', axis=0, tiled=True)]
    unnamed x9 -> x0, waiting for transfers between devices: 340 us -> none
    reduce_scatter x1 -> x0, waiting for transfers between devices: 152 us -> none  [shards(): lax.psum_scatter(jnp.dot(grad_logits, label_embed, preferred_element_type...]
    pallas_call x0 -> x1, Pallas kernels: none -> 96.2 us  [shards(): pl.pallas_call(kernel, out_shape=(jax.ShapeDtypeStruct((e_row, width), F3...]
    all_gather x1 -> x0, blocking collectives: 82.5 us -> none  [shards(): lax.all_gather(pos_ids, 'qry', axis=0, tiled=True)]
    dot_general x6 -> x0, matrix products: 38.8 us -> none  [the longest x1 9.79 us: shards(): lax.dot_general(label_hidden, grad_label_embed, (((0,), (0,)), ((), ())),...]
    unnamed x21 -> x4, local copies, waits for them, and re-layouts: 23.2 us -> 2.66 us
    reduce_sum x2 -> x0, other arithmetic: 20 us -> none  [the longest x1 12.7 us: shards(): label_loss = jnp.sum(loss_terms, axis=0) / n_query]
  transfers between devices with their start and end apart: 7 -> 0, of which waited for: 6 -> 0; matrix products, arithmetic and copies ran while one was open for 6% -> 0% of each run, Pallas kernels for 0% -> 0%
where the time goes in v3:
time: 99.6 us; the launch traced here: 99.5 us
  Pallas kernels  96.2 us (97%)
  local copies, waits for them, and re-layouts  2.66 us (3%)
    pallas_call x1, Pallas kernels, shards(): pl.pallas_call(kernel, out_shape=(jax.ShapeDtypeStruct((e_row, width), F3...  96.2 us
    unnamed x4, local copies, waits for them, and re-layouts  2.66 us

profile of v3, /device:TPU:0, one launch (start us, length us, event | category | flops | bytes accessed | tf_op | source)
XLA Modules:
  0.0 99.5 jit_solution(10172049504012130705)
XLA Ops:
  0.6 96.2 %focal_step.1 = (f32[112,896]{1,0:T(8,128)S(1)}, f32[48,896]{1,0:T(8,128)S(1)}, f32[1,1024]{1,0:T(1,128)S(1)}, f32[32,896]{1,0:T(8,128)S(1)}) custom-call(bf16[32,3584]{1,0:T(8,128)(2,1)} %refs_0_.1, bf16[112,896]{1,0:T(8,128)(2,1)} %refs_1_.1, bf16[1024,1536]{1,0:T(8,128)(2,1)} %refs_2_.1, bf16[48,896]{1,0:T(8,128)(2,1)} %refs_3_.1, s32[8,32]{1,0:T(8,128)} %bitcast.4, ...), custom_call_target="tpu_custom_call" | custom-call | tf_op jit(solution)/shard_map/focal_step/pallas_call | solution.py:610
  96.8 0.8 copy.14
  97.6 0.7 copy.15
  98.2 0.6 copy.16
  98.8 0.6 copy.17

commit v4 on v3

--- a/solution.py
+++ b/solution.py
@@ -49,6 +49,9 @@
 
     def next_lab(d):
         return lax.rem(j + d, NLAB)
+
+    def across(d):
+        return {**y_peer, "lab": next_lab(d)}
 
     def rows(index, size):
         return pl.ds(pl.multiple_of(index * size, size), size)
@@ -100,6 +103,7 @@
     each(NX, lambda d: greet(at(z, 1 - y, next_x(d))))
     each(NZ, lambda d: greet(at(next_z(d), 1 - y, x)))
     each(NLAB, lambda d: greet({"lab": next_lab(d)}))
+    each(NLAB, lambda d: greet(across(d)))
 
     loads[0].wait()
     for k in range(NX):
@@ -118,7 +122,7 @@
     s.ids_send[...] = jnp.full(s.ids_send.shape, -1, jnp.int32)
     slot_at = lax.broadcasted_iota(jnp.int32, ids.shape, 0)
     s.ids_send[:, :own] = jnp.where(slot_at < s.used[...], s.ids_raw[...], -1)
-    pl.semaphore_wait(barrier, 2 * (NX - 1) + 2 * (NZ - 1) + 1 + NLAB - 1)
+    pl.semaphore_wait(barrier, 2 * (NX - 1) + 2 * (NZ - 1) + 1 + 2 * (NLAB - 1))
 
     x_cols, z_cols = pl.ds(0, cut), pl.ds(cut, width - cut)
 
@@ -149,16 +153,21 @@
     def l_x(d):
         return push("l_x", d, lp, s.lp.at[y, x], at(z, y, next_x(d)))
 
+    def l_own(d):
+        return push("l_own", d, lp, s.lp.at[y, x], y_peer)
+
     def l_y(d):
-        return push("l_y", d, s.lp.at[y], s.lp.at[y], y_peer)
-
+        block_at = s.lp.at[y, lax.rem(x + NX - d, NX)]
+        return push("l_y", d, block_at, block_at, y_peer)
+
+    start(NX, l_x)
     start(2, w_yx)
     start(2, w_yz)
+    start(2, l_own)
     start(NX, w_x)
     start(NZ, w_z)
     start(NZ, q0)
     start(NX, q1)
-    start(NX, l_x)
 
     def i_y(d):
         return push("i_y", d, s.ids_send, s.ids.at[x, y], y_peer)
@@ -203,8 +212,7 @@
             each(NZ, lambda d: i_z(d).wait_send())
 
     arrive(NX, l_x)
-    loads[5].wait()
-    start(2, l_y)
+    start(NX, l_y)
 
     arrive(NZ, q0)
     arrive(NX, w_x)
@@ -258,27 +266,35 @@
         return push("q_all", d, s.qe.at[z], s.qe.at[z], at(next_z(d), y, x))
 
     start(NZ, q_all)
-    arrive(2, l_y)
+    loads[5].wait()
+    arrive(2, l_own)
+    arrive(NX, l_y)
     arrive(NZ, q_all)
 
-    s.t_part[...] = dot(s.qe[...].reshape(block, width), s.lp[...].reshape(d_z, width), COLS).reshape(NLAB, own, d_z)
+    part = dot(s.qe[...].reshape(block, width), s.lp[...].reshape(d_z, width), COLS)
+    s.t_part[...] = part.astype(BF16).reshape(NLAB, own, d_z)
 
     def t_sum(d):
-        return push("t_sum", d, s.t_part.at[next_lab(d)], s.t_recv.at[j], {"lab": next_lab(d)})
+        return push("t_sum", d, s.t_part.at[next_lab(d)], s.t_recv.at[y, j], {"lab": next_lab(d)})
+
+    def t_cross(d):
+        return push("t_cross", d, s.t_part.at[next_lab(d)], s.t_recv.at[y, j], across(d))
 
     start(NLAB, t_sum)
-    s.t_recv[j] = s.t_part[j]
+    start(NLAB + 1, t_cross)
+    s.t_recv[y, j] = s.t_part[j]
 
     arrive(NLAB, count)
     counts = jnp.sum(s.c_recv[0] + s.c_recv[1] + s.c_recv[2] + s.c_recv[3], axis=0, keepdims=True)
     s.weight[...] = (1.0 - 0.99) / (1.0 - jnp.exp((counts + 1.0) * float(np.log(np.float64(np.float32(0.99))))))
 
     arrive(NLAB, t_sum)
+    arrive(NLAB + 1, t_cross)
     mine = rows(z, d_z)
-    s.t[x, y, :, mine] = (s.t_recv[0] + s.t_recv[1] + s.t_recv[2] + s.t_recv[3]).astype(BF16)
-
-    def t_y(d):
-        return push("t_y", d, s.t.at[x, y, :, mine], s.t.at[x, y, :, mine], y_peer)
+    total = s.t_recv[:, 0].astype(F32)
+    for k in range(1, NLAB):
+        total += s.t_recv[:, k].astype(F32)
+    s.t[x, :, :, mine] = total.astype(BF16)
 
     def t_x(d):
         return push("t_x", d, s.t.at[x, 0, :, mine], s.t.at[x, 0, :, mine], at(z, y, next_x(d)))
@@ -292,8 +308,6 @@
     def t_zx(d):
         return push("t_zx", d, s.t.at[x, 1], s.t.at[x, 1], at(z, y, next_x(d)))
 
-    start(2, t_y)
-    arrive(2, t_y)
     start(NX, t_x)
     start(NZ, t_z)
     arrive(NX, t_x)
@@ -407,21 +421,23 @@
         half += s.u_rxz[next_z(d)].astype(F32)
     s.back[1] = half
 
-    def u_y(d):
-        return push("u_y", d, s.back.at[1 - y], s.u_peer, y_peer)
-
-    start(2, u_y)
-    arrive(2, u_y)
-    s.u[j] = (s.back[y] + s.u_peer[...]).astype(BF16)
+    s.u_send[...] = s.back[...].astype(BF16)
 
     def u_all(d):
-        return push("u_all", d, s.u.at[j], s.u.at[j], {"lab": next_lab(d)})
+        return push("u_all", d, s.u_send.at[y], s.u.at[y, j], {"lab": next_lab(d)})
+
+    def u_cross(d):
+        return push("u_cross", d, s.u_send.at[1 - y], s.u.at[y, j], across(d))
 
     start(NLAB, u_all)
+    start(NLAB + 1, u_cross)
+    s.u[y, j] = s.u_send[y]
     arrive(NLAB, u_all)
-    u = s.u[...].reshape(block, d_z)
-
-    part = dot(u, s.lp[...].reshape(d_z, width)).reshape(NZ, own, width)
+    arrive(NLAB + 1, u_cross)
+    u = [s.u[k].reshape(block, d_z) for k in range(NY)]
+
+    l_proj = s.lp[...].reshape(d_z, width)
+    part = (dot(u[0], l_proj) + dot(u[1], l_proj)).reshape(NZ, own, width)
     s.g_part[...] = part
     s.g_send[...] = part.astype(BF16)
 
@@ -429,7 +445,8 @@
         return push("g_sum", d, s.g_send.at[next_z(d)], s.g_recv.at[z], at(next_z(d), y, x))
 
     start(NZ, g_sum)
-    part = dot(u, s.qe[...].reshape(block, width), ROWS).reshape(NY, NX, d_row, width)
+    qe = s.qe[...].reshape(block, width)
+    part = (dot(u[0], qe, ROWS) + dot(u[1], qe, ROWS)).reshape(NY, NX, d_row, width)
     s.k_part[...] = part
     s.k_send[...] = part.astype(BF16)
 
@@ -444,16 +461,34 @@
     gqe_out[...] = total
     s.ge[...] = total.astype(BF16)
 
-    def g_bx(d):
-        nz, ny = in_b(d)
-        return push("g_bx", d, s.ge.at[:, x_cols], s.gx.at[spot_b], at(nz, ny, x))
-
-    def g_bz(d):
-        nx, ny = in_c(d)
-        return push("g_bz", d, s.ge.at[:, z_cols], s.gz.at[spot_c], at(z, ny, nx))
-
-    start(NZ * NY, g_bx)
-    start(NX * NY, g_bz)
+    def g_yx(d):
+        return push("g_yx", d, s.ge.at[:, x_cols], s.gx.at[spot_b], y_peer)
+
+    def g_yz(d):
+        return push("g_yz", d, s.ge.at[:, z_cols], s.gz.at[spot_c], y_peer)
+
+    def g_z(d):
+        return push("g_z", d, s.ge.at[:, x_cols], s.gx.at[spot_b], at(next_z(d), y, x))
+
+    def g_x(d):
+        return push("g_x", d, s.ge.at[:, z_cols], s.gz.at[spot_c], at(z, y, next_x(d)))
+
+    def g_fz(d):
+        other = s.gx.at[NY * z + 1 - y]
+        return push("g_fz", d, other, other, at(next_z(d), y, x))
+
+    def g_fx(d):
+        other = s.gz.at[NY * x + 1 - y]
+        return push("g_fx", d, other, other, at(z, y, next_x(d)))
+
+    start(2, g_yx)
+    start(2, g_yz)
+    start(NZ, g_z)
+    start(NX, g_x)
+    arrive(2, g_yx)
+    start(NZ, g_fz)
+    arrive(2, g_yz)
+    start(NX, g_fx)
     s.gx[spot_b] = s.ge[:, :cut]
     s.gz[spot_c] = s.ge[:, cut:]
     arrive(NLAB, loss_sum)
@@ -462,7 +497,8 @@
     arrive(NZ * NY, q_bx)
     arrive(NX * NY, q_bz)
 
-    arrive(NZ * NY, g_bx)
+    arrive(NZ, g_z)
+    arrive(NZ, g_fz)
     part = dot(s.qx[...].reshape(here, e_b), s.gx[...].reshape(here, cut), ROWS).reshape(NX, e_row, cut)
     s.px_part[...] = part
     s.px_send[...] = part.astype(BF16)
@@ -471,7 +507,8 @@
         return push("p_x", d, s.px_send.at[next_x(d)], s.px_recv.at[x], at(z, y, next_x(d)))
 
     start(NX, p_x)
-    arrive(NX * NY, g_bz)
+    arrive(NX, g_x)
+    arrive(NX, g_fx)
     part = dot(s.qz[...].reshape(here, e_b), s.gz[...].reshape(here, width - cut), ROWS).reshape(NZ, e_row, width - cut)
     s.pz_part[...] = part
     s.pz_send[...] = part.astype(BF16)
@@ -551,8 +588,8 @@
         "c_recv": ((NLAB, 8, n_label), F32),
         "weight": ((1, n_label), F32),
         "qe": ((NZ, own, width), BF16),
-        "t_part": ((NLAB, own, d_z), F32),
-        "t_recv": ((NLAB, own, d_z), F32),
+        "t_part": ((NLAB, own, d_z), BF16),
+        "t_recv": ((NY, NLAB, own, d_z), BF16),
         "t": ((NX, NY, own, wide_d), BF16),
         "logit": ((here, 256), F32),
         "gl": ((here, n_label), BF16),
@@ -566,8 +603,8 @@
         "u_rzx": ((NX, own, d_z), BF16),
         "u_rxz": ((NZ, own, d_z), BF16),
         "back": ((NY, own, d_z), F32),
-        "u_peer": ((own, d_z), F32),
-        "u": ((NLAB, own, d_z), BF16),
+        "u_send": ((NY, own, d_z), BF16),
+        "u": ((NY, NLAB, own, d_z), BF16),
         "g_part": ((NZ, own, width), F32),
         "g_send": ((NZ, own, width), BF16),
         "g_recv": ((NZ, own, width), BF16),
@@ -588,13 +625,13 @@
     }
     scratch = {name: pltpu.VMEM(*spec) for name, spec in scratch.items()}
     scratch["load"] = pltpu.SemaphoreType.DMA((7,))
-    pairs = ("w_yx", "w_yz", "l_y", "i_y", "t_y", "u_y", "k_y")
+    pairs = ("w_yx", "w_yz", "l_own", "i_y", "g_yx", "g_yz", "k_y")
     fours = (
-        "w_x", "w_z", "w_fx", "w_fz", "q0", "q1", "l_x", "i_x", "i_z", "b_z", "b_x", "count", "q_all", "t_sum",
-        "t_x", "t_z", "t_xz", "t_zx", "u_z", "u_x", "u_zx", "u_xz", "loss", "u_all", "g_sum", "k_x", "p_x", "p_z",
+        "w_x", "w_z", "w_fx", "w_fz", "q0", "q1", "l_x", "l_y", "i_x", "i_z", "b_z", "b_x", "count", "q_all", "t_sum",
+        "t_x", "t_z", "t_xz", "t_zx", "u_z", "u_x", "u_zx", "u_xz", "loss", "u_all", "g_sum", "g_z", "g_x", "g_fz", "g_fx", "k_x", "p_x", "p_z",
     )
-    eights = ("q_bx", "q_bz", "g_bx", "g_bz")
-    for number, group in ((2, pairs), (4, fours), (8, eights)):
+    fives, eights = ("t_cross", "u_cross"), ("q_bx", "q_bz")
+    for number, group in ((2, pairs), (4, fours), (5, fives), (8, eights)):
         for name in group:
             scratch["send_" + name] = pltpu.SemaphoreType.DMA((number,))
             scratch["recv_" + name] = pltpu.SemaphoreType.DMA((number,))

time: 99.6 us -> 95 us (0.954)
  Pallas kernels: 96.2 us -> 91.6 us
    pallas_call x1, Pallas kernels: 96.2 us -> 91.6 us  [shards(): pl.pallas_call(kernel, out_shape=(jax.ShapeDtypeStruct((e_row, width), F3...]
where the time goes in v4:
time: 95 us; the launch traced here: 94.9 us
  Pallas kernels  91.6 us (96%)
  local copies, waits for them, and re-layouts  2.66 us (3%)
    pallas_call x1, Pallas kernels, shards(): pl.pallas_call(kernel, out_shape=(jax.ShapeDtypeStruct((e_row, width), F3...  91.6 us
    unnamed x4, local copies, waits for them, and re-layouts  2.66 us

profile of v4, /device:TPU:0, one launch (start us, length us, event | category | flops | bytes accessed | tf_op | source)
XLA Modules:
  0.0 94.9 jit_solution(9223312327654621841)
XLA Ops:
  0.6 91.6 %focal_step.1 = (f32[112,896]{1,0:T(8,128)S(1)}, f32[48,896]{1,0:T(8,128)S(1)}, f32[1,1024]{1,0:T(1,128)S(1)}, f32[32,896]{1,0:T(8,128)S(1)}) custom-call(bf16[32,3584]{1,0:T(8,128)(2,1)} %refs_0_.1, bf16[112,896]{1,0:T(8,128)(2,1)} %refs_1_.1, bf16[1024,1536]{1,0:T(8,128)(2,1)} %refs_2_.1, bf16[48,896]{1,0:T(8,128)(2,1)} %refs_3_.1, s32[8,32]{1,0:T(8,128)} %bitcast.4, ...), custom_call_target="tpu_custom_call" | custom-call | tf_op jit(solution)/shard_map/focal_step/pallas_call | solution.py:647
  92.2 0.8 copy.14
  93.0 0.7 copy.15
  93.6 0.6 copy.16
  94.2 0.6 copy.17

commit v5 on v4

--- a/solution.py
+++ b/solution.py
@@ -302,21 +302,31 @@
     def t_z(d):
         return push("t_z", d, s.t.at[x, 1, :, mine], s.t.at[x, 1, :, mine], at(next_z(d), y, x))
 
-    def t_xz(d):
-        return push("t_xz", d, s.t.at[:, 0, :, mine], s.t.at[:, 0, :, mine], at(next_z(d), y, x))
-
-    def t_zx(d):
-        return push("t_zx", d, s.t.at[x, 1], s.t.at[x, 1], at(z, y, next_x(d)))
+    def t_xz(k):
+        tile = s.t.at[lax.rem(x + NX - k, NX), 0, :, mine]
+        return lambda d: push("t_xz", NZ * k + d, tile, tile, at(next_z(d), y, x))
+
+    def t_zx(k):
+        tile = s.t.at[x, 1, :, rows(lax.rem(z + NZ - k, NZ), d_z)]
+        return lambda d: push("t_zx", NX * k + d, tile, tile, at(z, y, next_x(d)))
+
+    def q_y(d):
+        return push("q_y", d, s.qe, s.qe_peer, y_peer)
 
     start(NX, t_x)
     start(NZ, t_z)
-    arrive(NX, t_x)
-    start(NZ, t_xz)
-    arrive(NZ, t_z)
-    start(NX, t_zx)
+    start(NZ, t_xz(0))
+    start(NX, t_zx(0))
+    for k in range(1, NX):
+        t_x(k).wait_recv()
+        start(NZ, t_xz(k))
+        t_z(k).wait_recv()
+        start(NX, t_zx(k))
+    start(2, q_y)
     loads[6].wait()
-    arrive(NZ, t_xz)
-    arrive(NX, t_zx)
+    for k in range(NX):
+        arrive(NZ, t_xz(k))
+        arrive(NX, t_zx(k))
 
     def in_b(d):
         return lax.rem(z + lax.div(d, NY), NZ), lax.rem(y + lax.rem(d, NY), NY)
@@ -436,6 +446,12 @@
     arrive(NLAB + 1, u_cross)
     u = [s.u[k].reshape(block, d_z) for k in range(NY)]
 
+    s.u_sum[...] = (u[0].astype(F32) + u[1].astype(F32)).astype(BF16)
+
+    def u_y(d):
+        return push("u_y", d, s.u_sum, s.u_peer, y_peer)
+
+    start(2, u_y)
     l_proj = s.lp[...].reshape(d_z, width)
     part = (dot(u[0], l_proj) + dot(u[1], l_proj)).reshape(NZ, own, width)
     s.g_part[...] = part
@@ -445,13 +461,17 @@
         return push("g_sum", d, s.g_send.at[next_z(d)], s.g_recv.at[z], at(next_z(d), y, x))
 
     start(NZ, g_sum)
+
     qe = s.qe[...].reshape(block, width)
-    part = (dot(u[0], qe, ROWS) + dot(u[1], qe, ROWS)).reshape(NY, NX, d_row, width)
-    s.k_part[...] = part
-    s.k_send[...] = part.astype(BF16)
+    part = dot(u[0], qe, ROWS) + dot(u[1], qe, ROWS)
+    arrive(2, q_y)
+    arrive(2, u_y)
+    part += dot(s.u_peer[...], s.qe_peer[...].reshape(block, width), ROWS)
+    s.k_both[...] = part.reshape(NY, NX, d_row, width)
+    s.k_send[...] = s.k_both[y].astype(BF16)
 
     def k_x(d):
-        return push("k_x", d, s.k_send.at[:, next_x(d)], s.k_recv.at[x], at(z, y, next_x(d)))
+        return push("k_x", d, s.k_send.at[next_x(d)], s.k_recv.at[x], at(z, y, next_x(d)))
 
     start(NX, k_x)
     arrive(NZ, g_sum)
@@ -519,22 +539,15 @@
     start(NZ, p_z)
 
     arrive(NX, k_x)
-    total = s.k_part[:, x]
+    total = s.k_both[y, x]
     for d in range(1, NX):
         total += s.k_recv[next_x(d)].astype(F32)
-    s.k_sum[...] = total
-
-    def k_y(d):
-        return push("k_y", d, s.k_sum.at[1 - y], s.k_peer, y_peer)
-
-    start(2, k_y)
+    glp_out[...] = total
     arrive(NX, p_x)
     total = s.px_part[x]
     for d in range(1, NX):
         total += s.px_recv[next_x(d)].astype(F32)
     gqp_out[:, :cut] = total
-    arrive(2, k_y)
-    glp_out[...] = s.k_sum[y] + s.k_peer[...]
     arrive(NZ, p_z)
     total = s.pz_part[z]
     for d in range(1, NZ):
@@ -559,7 +572,7 @@
     d_row = label_proj.shape[0]
     slots = pos_ids.shape[1]
     e_z, d_z, e_b = NX * NY * e_row, NX * NY * d_row, NX * e_row
-    here = NX * NY * own
+    here, block = NX * NY * own, NZ * own
     cut = width // 256 * 128
     rest = width - cut
     scratch = {
@@ -605,17 +618,18 @@
         "back": ((NY, own, d_z), F32),
         "u_send": ((NY, own, d_z), BF16),
         "u": ((NY, NLAB, own, d_z), BF16),
+        "u_sum": ((block, d_z), BF16),
+        "u_peer": ((block, d_z), BF16),
+        "qe_peer": ((NZ, own, width), BF16),
         "g_part": ((NZ, own, width), F32),
         "g_send": ((NZ, own, width), BF16),
         "g_recv": ((NZ, own, width), BF16),
         "ge": ((own, width), BF16),
         "gx": ((NZ * NY, own, cut), BF16),
         "gz": ((NX * NY, own, rest), BF16),
-        "k_part": ((NY, NX, d_row, width), F32),
-        "k_send": ((NY, NX, d_row, width), BF16),
-        "k_recv": ((NX, NY, d_row, width), BF16),
-        "k_sum": ((NY, d_row, width), F32),
-        "k_peer": ((d_row, width), F32),
+        "k_both": ((NY, NX, d_row, width), F32),
+        "k_send": ((NX, d_row, width), BF16),
+        "k_recv": ((NX, d_row, width), BF16),
         "px_part": ((NX, e_row, cut), F32),
         "px_send": ((NX, e_row, cut), BF16),
         "px_recv": ((NX, e_row, cut), BF16),
@@ -625,13 +639,14 @@
     }
     scratch = {name: pltpu.VMEM(*spec) for name, spec in scratch.items()}
     scratch["load"] = pltpu.SemaphoreType.DMA((7,))
-    pairs = ("w_yx", "w_yz", "l_own", "i_y", "g_yx", "g_yz", "k_y")
+    pairs = ("w_yx", "w_yz", "l_own", "i_y", "g_yx", "g_yz", "q_y", "u_y")
     fours = (
         "w_x", "w_z", "w_fx", "w_fz", "q0", "q1", "l_x", "l_y", "i_x", "i_z", "b_z", "b_x", "count", "q_all", "t_sum",
-        "t_x", "t_z", "t_xz", "t_zx", "u_z", "u_x", "u_zx", "u_xz", "loss", "u_all", "g_sum", "g_z", "g_x", "g_fz", "g_fx", "k_x", "p_x", "p_z",
+        "t_x", "t_z", "u_z", "u_x", "u_zx", "u_xz", "loss", "u_all", "g_sum", "g_z", "g_x", "g_fz", "g_fx", "k_x", "p_x", "p_z",
     )
     fives, eights = ("t_cross", "u_cross"), ("q_bx", "q_bz")
-    for number, group in ((2, pairs), (4, fours), (5, fives), (8, eights)):
+    sixteens = ("t_xz", "t_zx")
+    for number, group in ((2, pairs), (4, fours), (5, fives), (8, eights), (16, sixteens)):
         for name in group:
             scratch["send_" + name] = pltpu.SemaphoreType.DMA((number,))
             scratch["recv_" + name] = pltpu.SemaphoreType.DMA((number,))

time: 95 us -> 93.1 us (0.980)
  Pallas kernels: 91.6 us -> 89.7 us
    pallas_call x1, Pallas kernels: 91.6 us -> 89.7 us  [shards(): pl.pallas_call(kernel, out_shape=(jax.ShapeDtypeStruct((e_row, width), F3...]
where the time goes in v5:
time: 93.1 us; the launch traced here: 93 us
  Pallas kernels  89.7 us (96%)
  local copies, waits for them, and re-layouts  2.66 us (3%)
    pallas_call x1, Pallas kernels, shards(): pl.pallas_call(kernel, out_shape=(jax.ShapeDtypeStruct((e_row, width), F3...  89.7 us
    unnamed x4, local copies, waits for them, and re-layouts  2.66 us

profile of v5, /device:TPU:0, one launch (start us, length us, event | category | flops | bytes accessed | tf_op | source)
XLA Modules:
  0.0 93.0 jit_solution(12749892513982921298)
XLA Ops:
  0.6 89.7 %focal_step.1 = (f32[112,896]{1,0:T(8,128)S(1)}, f32[48,896]{1,0:T(8,128)S(1)}, f32[1,1024]{1,0:T(1,128)S(1)}, f32[32,896]{1,0:T(8,128)S(1)}) custom-call(bf16[32,3584]{1,0:T(8,128)(2,1)} %refs_0_.1, bf16[112,896]{1,0:T(8,128)(2,1)} %refs_1_.1, bf16[1024,1536]{1,0:T(8,128)(2,1)} %refs_2_.1, bf16[48,896]{1,0:T(8,128)(2,1)} %refs_3_.1, s32[8,32]{1,0:T(8,128)} %bitcast.4, ...), custom_call_target="tpu_custom_call" | custom-call | tf_op jit(solution)/shard_map/focal_step/pallas_call | solution.py:662
  90.4 0.8 copy.14
  91.1 0.7 copy.15
  91.8 0.6 copy.16
  92.4 0.6 copy.17

commit v6 on v5

--- a/solution.py
+++ b/solution.py
@@ -19,11 +19,8 @@
 
 
 def each(count, step):
-    def body(d, carry):
+    for d in range(1, count):
         step(d)
-        return carry
-
-    lax.fori_loop(1, count, body, 0)
 
 
 def step_kernel(temper, cut, qh, qp, lh, lp, ids, used, gqp_out, glp_out, loss_out, gqe_out, s):
@@ -322,7 +319,6 @@
         start(NZ, t_xz(k))
         t_z(k).wait_recv()
         start(NX, t_zx(k))
-    start(2, q_y)
     loads[6].wait()
     for k in range(NX):
         arrive(NZ, t_xz(k))
@@ -349,6 +345,7 @@
     s.qx[spot_b] = s.qx_send[spot_b]
     s.qz[spot_c] = s.qz_send[spot_c]
 
+    start(2, q_y)
     tall = 32
 
     def label_block(c, carry):
@@ -372,7 +369,7 @@
             s.gl[some, cols] = jnp.where(hit, -slope, slope).astype(BF16)
             return loss + jnp.sum((weight * (square * soft)).reshape(tall // 8, 8, wide), axis=0)
 
-        s.l_part[:, cols] = lax.fori_loop(0, here // tall, row_block, jnp.zeros((8, wide), F32))
+        s.l_part[:, cols] = lax.fori_loop(0, here // tall, row_block, jnp.zeros((8, wide), F32), unroll=True)
         return carry
 
     lax.fori_loop(0, n_label // wide, label_block, 0)

time: 93.1 us -> 91.3 us (0.981)
  Pallas kernels: 89.7 us -> 87.4 us
    pallas_call x1, Pallas kernels: 89.7 us -> 87.4 us  [shards(): pl.pallas_call(kernel, out_shape=(jax.ShapeDtypeStruct((e_row, width), F3...]
where the time goes in v6:
time: 91.3 us; the launch traced here: 90.7 us
  Pallas kernels  87.4 us (96%)
  local copies, waits for them, and re-layouts  2.66 us (3%)
    pallas_call x1, Pallas kernels, shards(): pl.pallas_call(kernel, out_shape=(jax.ShapeDtypeStruct((e_row, width), F3...  87.4 us
    unnamed x4, local copies, waits for them, and re-layouts  2.66 us

profile of v6, /device:TPU:0, one launch (start us, length us, event | category | flops | bytes accessed | tf_op | source)
XLA Modules:
  0.0 90.7 jit_solution(2501507995182563044)
XLA Ops:
  0.6 87.4 %focal_step.1 = (f32[112,896]{1,0:T(8,128)S(1)}, f32[48,896]{1,0:T(8,128)S(1)}, f32[1,1024]{1,0:T(1,128)S(1)}, f32[32,896]{1,0:T(8,128)S(1)}) custom-call(bf16[32,3584]{1,0:T(8,128)(2,1)} %refs_0_.1, bf16[112,896]{1,0:T(8,128)(2,1)} %refs_1_.1, bf16[1024,1536]{1,0:T(8,128)(2,1)} %refs_2_.1, bf16[48,896]{1,0:T(8,128)(2,1)} %refs_3_.1, s32[8,32]{1,0:T(8,128)} %bitcast.4, ...), custom_call_target="tpu_custom_call" | custom-call | tf_op jit(solution)/shard_map/focal_step/pallas_call | solution.py:659
  88.1 0.8 copy.14
  88.8 0.7 copy.15
  89.5 0.6 copy.16
  90.1 0.6 copy.17

commit v7 on v6

--- a/solution.py
+++ b/solution.py
@@ -281,10 +281,6 @@
     start(NLAB + 1, t_cross)
     s.t_recv[y, j] = s.t_part[j]
 
-    arrive(NLAB, count)
-    counts = jnp.sum(s.c_recv[0] + s.c_recv[1] + s.c_recv[2] + s.c_recv[3], axis=0, keepdims=True)
-    s.weight[...] = (1.0 - 0.99) / (1.0 - jnp.exp((counts + 1.0) * float(np.log(np.float64(np.float32(0.99))))))
-
     arrive(NLAB, t_sum)
     arrive(NLAB + 1, t_cross)
     mine = rows(z, d_z)
@@ -319,6 +315,10 @@
         start(NZ, t_xz(k))
         t_z(k).wait_recv()
         start(NX, t_zx(k))
+    arrive(NLAB, count)
+    counts = jnp.sum(s.c_recv[0] + s.c_recv[1] + s.c_recv[2] + s.c_recv[3], axis=0, keepdims=True)
+    s.weight[...] = (1.0 - 0.99) / (1.0 - jnp.exp((counts + 1.0) * float(np.log(np.float64(np.float32(0.99))))))
+
     loads[6].wait()
     for k in range(NX):
         arrive(NZ, t_xz(k))

time: 91.3 us -> 91.3 us (level)
  no operation moved by 1% of the time
where the time goes in v7:
time: 91.3 us; the launch traced here: 90.7 us
  Pallas kernels  87.4 us (96%)
  local copies, waits for them, and re-layouts  2.66 us (3%)
    pallas_call x1, Pallas kernels, shards(): pl.pallas_call(kernel, out_shape=(jax.ShapeDtypeStruct((e_row, width), F3...  87.4 us
    unnamed x4, local copies, waits for them, and re-layouts  2.66 us

profile of v7, /device:TPU:0, one launch (start us, length us, event | category | flops | bytes accessed | tf_op | source)
XLA Modules:
  0.0 90.7 jit_solution(17170378113723050159)
XLA Ops:
  0.6 87.4 %focal_step.1 = (f32[112,896]{1,0:T(8,128)S(1)}, f32[48,896]{1,0:T(8,128)S(1)}, f32[1,1024]{1,0:T(1,128)S(1)}, f32[32,896]{1,0:T(8,128)S(1)}) custom-call(bf16[32,3584]{1,0:T(8,128)(2,1)} %refs_0_.1, bf16[112,896]{1,0:T(8,128)(2,1)} %refs_1_.1, bf16[1024,1536]{1,0:T(8,128)(2,1)} %refs_2_.1, bf16[48,896]{1,0:T(8,128)(2,1)} %refs_3_.1, s32[8,32]{1,0:T(8,128)} %bitcast.4, ...), custom_call_target="tpu_custom_call" | custom-call | tf_op jit(solution)/shard_map/focal_step/pallas_call | solution.py:659
  88.1 0.8 copy.14
  88.8 0.7 copy.15
  89.5 0.6 copy.16
  90.1 0.6 copy.17
